TPU v7x, 128 devices: a whole 4x4x4 slice. The times are simulated.
128 devices in a mesh: row: 128 (over y, x, z, core).
Axes of the slice: x: 4, y: 4, z: 4, core: 2. Of those that a mesh axis runs over, the one named last changes fastest.
Arguments:
- displacement: float32 [512, 256, 2, 384], P('row'), may hold values from -6 to 6
- stiffness: bfloat16 [384, 384], replicated, may hold values from -0.3125 to 0.3125
- coupling: float32 [384], replicated, may hold values from 0.1 to 0.5
- softening: float32 [384], replicated, may hold values from 0.2 to 2
- electrode_mask: int32 [512, 256], P('row'), may hold values 0 or 1
- row_counts: int32 [128], replicated, may hold values from 1 to 4, 256 in all
- green_spectrum: float32 [4096, 4096], P('row'), may hold values from 0.25 to 1.25, as said below
Outputs:
- load_block: float32 [512, 256, 2, 384], P('row')
Inputs may be any that keep to these rules, and one draw needn't show every extreme that they name: Device d holds row_counts[d] cell rows, following those of the devices before it; the entries sum to 256. `electrode_mask`: entries of unused slots are not read. green_spectrum equals its transpose, and green_spectrum[kx, ky] = green_spectrum[-kx mod 4096, ky] = green_spectrum[kx, -ky mod 4096].
All inputs are finite; a program needn't handle non-finite values. No bound on the sum of `electrode_mask` on one device may be relied on, other than what follows from the above.
Results may differ from a plain program's by a relative error of at most 0.0021.
Values sent between devices are 32-bit elements; how exact they have to be, the bound alone decides.
No kernel may reach another device: no remote copies, remote signals or barrier semaphores. Data moves between devices by JAX's collectives and lax.ppermute only.
A program may use at most 128 MiB of HBM per device.

v0:
```python
import math

import jax
import jax.numpy as jnp
from jax import lax
from jax.sharding import PartitionSpec as P

FA = 64
FB = 64
CELL = 8


def with_halo(array, sides, width):
    for axis, dim in sides:
        devices, length = (lax.axis_size(axis), array.shape[dim])
        up = [(i, (i + 1) % devices) for i in range(devices - 1)]
        down = [(j, i) for i, j in up]
        last = lax.slice_in_dim(array, length - width, length, axis=dim)
        first = lax.slice_in_dim(array, 0, width, axis=dim)
        before = lax.ppermute(last, axis, up)
        after = lax.ppermute(first, axis, down)
        array = jnp.concatenate([before, array, after], axis=dim)
    return array


def angles(height, breadth, length):
    products = (
        jnp.arange(height, dtype=jnp.int32)[:, None]
        * jnp.arange(breadth, dtype=jnp.int32)[None, :]
        % length
    )
    phases = products.astype(jnp.float32) * (2.0 * math.pi / length)
    return (jnp.cos(phases), jnp.sin(phases))


def apply_left(matrix, values, pattern):
    return jnp.einsum(pattern, matrix, values, precision=lax.Precision.HIGHEST)


def forward_transform(real_part, imag_part):
    leading = real_part.shape[:-1]
    halved = FA // 2
    pattern = "kn,...nm->...km"
    real_in = real_part.reshape(leading + (halved, FB))
    cos_one, sin_one = angles(FA, halved, FA)
    first_re = apply_left(cos_one, real_in, pattern)
    first_im = -apply_left(sin_one, real_in, pattern)
    if imag_part is not None:
        imag_in = imag_part.reshape(leading + (halved, FB))
        first_re = first_re + apply_left(sin_one, imag_in, pattern)
        first_im = first_im + apply_left(cos_one, imag_in, pattern)
    cos_turn, sin_turn = angles(FA, FB, FA * FB)
    turned_re = first_re * cos_turn + first_im * sin_turn
    turned_im = first_im * cos_turn - first_re * sin_turn
    cos_two, sin_two = angles(FB, FB, FB)
    second = "jm,...km->...jk"
    out_re = apply_left(cos_two, turned_re, second) + apply_left(sin_two, turned_im, second)
    out_im = apply_left(cos_two, turned_im, second) - apply_left(sin_two, turned_re, second)
    return (out_re.reshape(leading + (FA * FB,)), out_im.reshape(leading + (FA * FB,)))


def inverse_transform(real_part, imag_part, keep_imag):
    leading = real_part.shape[:-1]
    halved = FA // 2
    spectral_re = real_part.reshape(leading + (FB, FA))
    spectral_im = imag_part.reshape(leading + (FB, FA))
    cos_two, sin_two = angles(FB, FB, FB)
    first = "mj,...jk->...km"
    middle_re = apply_left(cos_two, spectral_re, first) - apply_left(sin_two, spectral_im, first)
    middle_im = apply_left(cos_two, spectral_im, first) + apply_left(sin_two, spectral_re, first)
    cos_turn, sin_turn = angles(FA, FB, FA * FB)
    turned_re = middle_re * cos_turn - middle_im * sin_turn
    turned_im = middle_im * cos_turn + middle_re * sin_turn
    cos_one, sin_one = angles(halved, FA, FA)
    second = "nk,...km->...nm"
    out_re = apply_left(cos_one, turned_re, second) - apply_left(sin_one, turned_im, second)
    if keep_imag:
        out_im = apply_left(cos_one, turned_im, second) + apply_left(sin_one, turned_re, second)
        return (out_re.reshape(leading + (halved * FB,)), out_im.reshape(leading + (halved * FB,)))
    return out_re.reshape(leading + (halved * FB,))


def per_device(
    displacement, stiffness, coupling, softening, electrode_mask, row_counts, green_spectrum
):
    devices = lax.axis_size("row")
    position = lax.axis_index("row")
    slots, cell_count, columns, dof_count = displacement.shape
    surface_dofs = CELL * CELL
    grid_points = cell_count * CELL
    padded_points = 2 * grid_points
    slot_height = slots * CELL
    own_count = row_counts[position]
    starts = jnp.cumsum(row_counts) - row_counts
    slot_range = jnp.arange(slots, dtype=jnp.int32)
    used_slot = slot_range < own_count
    rounded = displacement.astype(jnp.bfloat16)
    elastic = jnp.dot(
        rounded.reshape(-1, dof_count), stiffness, preferred_element_type=jnp.float32
    ).reshape(displacement.shape)
    last_used = lax.dynamic_slice_in_dim(displacement, own_count - 1, 1, 0)
    rim_rows = jnp.concatenate([displacement[:1], last_used], axis=0)
    framed = with_halo(rim_rows, (("row", 0),), 1)
    from_above = jnp.concatenate([framed[0:1], displacement[:-1]], axis=0)
    shifted = jnp.concatenate([displacement[1:], jnp.zeros_like(displacement[:1])], axis=0)
    from_below = jnp.where((slot_range == own_count - 1)[:, None, None, None], framed[3:4], shifted)
    sideways = jnp.pad(displacement, ((0, 0), (1, 1), (0, 0), (0, 0)))
    beside = from_above + from_below + sideways[:, :-2] + sideways[:, 2:]
    electrode = electrode_mask.astype(jnp.float32)[:, :, None, None]
    structural = elastic - coupling * beside - electrode * softening * displacement
    surface = jnp.where(used_slot[:, None, None, None], displacement[..., :surface_dofs], 0.0)
    surface = surface.reshape(slots, cell_count, columns, CELL, CELL).transpose(2, 0, 3, 1, 4)
    surface = surface.reshape(columns, slot_height, grid_points)
    grid_rows = jnp.arange(grid_points, dtype=jnp.int32)
    cell_rows = grid_rows // CELL
    owners = jnp.sum((starts[None, :] <= cell_rows[:, None]).astype(jnp.int32), axis=1) - 1
    gather_rows = (owners * slots + cell_rows - starts[owners]) * CELL + grid_rows % CELL
    slot_rows = jnp.arange(devices * slot_height, dtype=jnp.int32)
    slot_device = slot_rows // slot_height
    slot_place = slot_rows // CELL % slots
    slot_used = slot_place < row_counts[slot_device]
    grid_of_slot = jnp.minimum(
        (starts[slot_device] + slot_place) * CELL + slot_rows % CELL, grid_points - 1
    )
    scale = 1.0 / float(padded_points * padded_points)

    def compact(values):
        return jnp.take(values, gather_rows, axis=1)

    def expand(values):
        return jnp.where(slot_used[None, :, None], jnp.take(values, grid_of_slot, axis=1), 0.0)

    real_part, imag_part = forward_transform(surface, None)
    real_part, imag_part = (
        lax.all_to_all(real_part, "row", split_axis=2, concat_axis=1, tiled=True),
        lax.all_to_all(imag_part, "row", split_axis=2, concat_axis=1, tiled=True),
    )
    real_part = jnp.swapaxes(compact(real_part), 1, 2)
    imag_part = jnp.swapaxes(compact(imag_part), 1, 2)
    real_part, imag_part = forward_transform(real_part, imag_part)
    real_part = real_part * green_spectrum
    imag_part = imag_part * green_spectrum
    real_part, imag_part = inverse_transform(real_part, imag_part, True)
    real_part = expand(jnp.swapaxes(real_part, 1, 2))
    imag_part = expand(jnp.swapaxes(imag_part, 1, 2))
    real_part, imag_part = (
        lax.all_to_all(real_part, "row", split_axis=1, concat_axis=2, tiled=True),
        lax.all_to_all(imag_part, "row", split_axis=1, concat_axis=2, tiled=True),
    )
    pressure = inverse_transform(real_part, imag_part, False) * scale
    pressure_dofs = pressure.reshape(columns, slots, CELL, cell_count, CELL).transpose(
        1, 3, 0, 2, 4
    )
    pressure_dofs = pressure_dofs.reshape(slots, cell_count, columns, surface_dofs)
    load_block = jnp.concatenate(
        [structural[..., :surface_dofs] + pressure_dofs, structural[..., surface_dofs:]], axis=-1
    )
    return jnp.where(used_slot[:, None, None, None], load_block, 0.0)


def solution(mesh):
    placed = (P("row", None, None, None), P(), P(), P(), P("row", None), P(), P("row", None))
    return jax.shard_map(
        per_device,
        mesh=mesh,
        in_specs=placed,
        out_specs=P("row", None, None, None),
        check_vma=False,
    )
```

profile of v0, /device:TPU:1, one launch (start us, length us, event | category | flops | bytes accessed | tf_op | source)
XLA Modules:
  0.0 595.1 jit_solution(1218726568476261334)
XLA Ops:
  32.5 6.9 %copy.259 = f32[2,32,64,64]{1,0,3,2:T(2,128)} copy(f32[2,32,64,64]{2,3,1,0:T(8,128)} %add_bitcast_fusion) | data formatting | bytes 2097152 | tf_op jit(solution)/shard_map/reshape | solution.py:59
  39.4 6.5 %reshape.330 = f32[128,1,2048]{2,1,0:T(1,128)} reshape(f32[4096,2,32]{2,1,0:T(2,128)} %bitcast.230) | data formatting | bytes 2097152
  45.9 12.0 %all-to-all-start = ((f32[128,1,2048]{2,1,0:T(1,128)}), f32[128,1,2048]{2,1,0:T(1,128)}, u32[]{:S(2)}, u32[]{:S(2)}) async-start(f32[128,1,2048]{2,1,0:T(1,128)} %reshape.330), calls=%async_computation | async-start | bytes 2097152 | tf_op jit(solution)/shard_map/all_to_all | solution.py:135
  57.9 6.6 %fusion.42 = f32[2,32,64,64]{3,2,1,0:T(8,128)} fusion(f32[2,32,64,64]{3,2,1,0:T(8,128)S(1)} %fusion.109, f32[2,32,64,64]{3,2,1,0:T(8,128)} %fusion.114, f32[64,64]{0,1:T(8,128)S(1)} %copy.175, f32[64,64]{0,1:T(8,128)S(1)} %copy.174), kind=kOutput, calls=%fused_computation.75 | convolution fusion | flops 202432512 | bytes 3178496 | tf_op jit(solution)/shard_map/jm,...km->...jk/dot_general | solution.py:37
  64.9 7.2 %subtract_bitcast_fusion = f32[2,32,64,64]{2,3,1,0:T(8,128)} fusion(f32[2,32,64,64]{3,2,1,0:T(8,128)} %fusion.42, f32[2,32,64,64]{3,2,1,0:T(8,128)S(1)} %fusion.109, f32[2,32,64,64]{3,2,1,0:T(8,128)} %fusion.114, f32[64,64]{0,1:T(8,128)S(1)} %copy.175, f32[64,64]{0,1:T(8,128)S(1)} %copy.174), kind=kOutput, calls=%fused_computation.45 | convolution fusion | flops 202694656 | bytes 4227072 | tf_op jit(solution)/shard_map/jm,...km->...jk/dot_general | solution.py:37
  72.1 6.9 %copy.263 = f32[2,32,64,64]{1,0,3,2:T(2,128)} copy(f32[2,32,64,64]{2,3,1,0:T(8,128)} %subtract_bitcast_fusion) | data formatting | bytes 2097152 | tf_op jit(solution)/shard_map/reshape | solution.py:59
  78.9 6.5 %reshape.332 = f32[128,1,2048]{2,1,0:T(1,128)} reshape(f32[4096,2,32]{2,1,0:T(2,128)} %bitcast.231) | data formatting | bytes 2097152
  85.5 42.4 %gather_fusion = s32[4096]{0:T(1024)} fusion(s32[128]{0:T(128)S(1)} %copy-done.1, s32[4096]{0:T(1024)S(1)} %broadcast_clamp_fusion.1), kind=kCustom, calls=%fused_computation.4 | custom fusion | bytes 49152 | tf_op jit(solution)/shard_map/gather | solution.py:121
  127.8 24.7 %gather_fusion.2 = s32[4096]{0:T(1024)S(1)} fusion(s32[128]{0:T(128)S(1)} %sub.90, s32[4096]{0:T(1024)S(1)} %broadcast_clamp_fusion.1), kind=kCustom, calls=%fused_computation.6 | custom fusion | bytes 49152 | tf_op jit(solution)/shard_map/gather | solution.py:123
  153.2 9.8 %all-to-all-start.1 = ((f32[128,1,2048]{2,1,0:T(1,128)}), f32[128,1,2048]{2,1,0:T(1,128)S(1)}, u32[]{:S(2)}, u32[]{:S(2)}) async-start(f32[128,1,2048]{2,1,0:T(1,128)} %reshape.332), calls=%async_computation.1 | async-start | bytes 2097152 | tf_op jit(solution)/shard_map/all_to_all | solution.py:136
  163.0 12.6 %gather_fusion.1 = s32[2048]{0:T(1024)S(1)} fusion(s32[128]{0:T(128)S(1)} %sub.90, s32[2048]{0:T(1024)S(1)} %broadcast_clamp_fusion.3), kind=kCustom, calls=%fused_computation.5 | custom fusion | bytes 24576 | tf_op jit(solution)/shard_map/gather | solution.py:117
  187.6 6.6 %copy.287 = f32[2,32,128,32]{1,2,3,0:T(8,128)} copy(f32[2,32,128,32]{1,0,3,2:T(2,128)} %bitcast.232) | data formatting | bytes 2097152 | tf_op jit(solution)/shard_map/all_to_all | solution.py:135
  194.2 7.4 %copy.262 = f32[2,128,32,32]{3,0,2,1:T(2,128)} copy(f32[2,128,32,32]{2,1,3,0:T(8,128)} %bitcast.236) | data formatting | bytes 2097152 | tf_op jit(solution)/shard_map/all_to_all | solution.py:135
  210.2 6.6 %copy.286 = f32[2,32,128,32]{1,2,3,0:T(8,128)} copy(f32[2,32,128,32]{1,0,3,2:T(2,128)} %bitcast.233) | data formatting | bytes 2097152 | tf_op jit(solution)/shard_map/all_to_all | solution.py:136
  216.8 7.5 %copy.266 = f32[2,128,32,32]{3,0,2,1:T(2,128)} copy(f32[2,128,32,32]{2,1,3,0:T(8,128)} %bitcast.237) | data formatting | bytes 2097152 | tf_op jit(solution)/shard_map/all_to_all | solution.py:136
  224.2 16.7 %gather_fusion.3 = f32[2048,2,32]{2,1,0:T(2,128)} fusion(f32[2,4096,32]{2,0,1:T(2,128)} %bitcast.242, s32[2048]{0:T(1024)S(1)} %broadcast_clamp_fusion.2), kind=kCustom, calls=%fused_computation.clone | custom fusion | bytes 1056768 | tf_op jit(solution)/shard_map/jit(_take)/gather | solution.py:128
  240.9 16.7 %gather_fusion.4 = f32[2048,2,32]{2,1,0:T(2,128)} fusion(f32[2,4096,32]{2,0,1:T(2,128)} %bitcast.243, s32[2048]{0:T(1024)S(1)} %broadcast_clamp_fusion.2), kind=kCustom, calls=%fused_computation.2.clone | custom fusion | bytes 1056768 | tf_op jit(solution)/shard_map/jit(_take)/gather | solution.py:128
  257.6 11.1 %broadcast_select_fusion = (f32[2048,2,32]{2,1,0:T(2,128)}, f32[2048,2,32]{2,1,0:T(2,128)}) fusion(f32[2048,2,32]{2,1,0:T(2,128)} %gather_fusion.4, pred[2048]{0:T(1024)(128)(4,1)S(1)} %copy-done.15, f32[2048,2,32]{2,1,0:T(2,128)} %gather_fusion.3), kind=kLoop, calls=%fused_computation.47 | loop fusion | flops 262144 | bytes 2099200 | tf_op jit(solution)/shard_map/jit(_take)/select_n | solution.py:128
  304.2 6.1 %fusion.69 = f32[2,32,64,64]{2,3,1,0:T(8,128)S(1)} fusion(f32[2,32,64,64]{2,3,1,0:T(8,128)S(1)} %bitcast_multiply_fusion), kind=kOutput, calls=%fused_computation.103 | convolution fusion | flops 201383936 | bytes 2097152 | tf_op jit(solution)/shard_map/mj,...jk->...km/dot_general | solution.py:37
  320.6 6.2 %convolution_add_fusion.1 = f32[2,32,64,64]{2,3,1,0:T(8,128)S(1)} fusion(f32[2,32,64,64]{2,3,1,0:T(8,128)S(1)} %fusion.69, f32[2,32,64,64]{2,3,1,0:T(8,128)S(1)} %bitcast_multiply_fusion.1), kind=kOutput, calls=%fused_computation.51 | convolution fusion | flops 201646080 | bytes 3145728 | tf_op jit(solution)/shard_map/mj,...jk->...km/dot_general | solution.py:37
  326.8 6.1 %convolution_subtract_fusion.1 = f32[2,32,64,64]{2,3,1,0:T(8,128)S(1)} fusion(f32[2,32,64,64]{2,3,1,0:T(8,128)S(1)} %fusion.72, f32[2,32,64,64]{2,3,1,0:T(8,128)S(1)} %bitcast_multiply_fusion), kind=kOutput, calls=%fused_computation.52 | convolution fusion | flops 201646080 | bytes 3145728 | tf_op jit(solution)/shard_map/mj,...jk->...km/dot_general | solution.py:37
  338.9 6.9 %fusion.35 = f32[2,32,64,32]{2,3,1,0:T(8,128)} fusion(f32[2,32,64,64]{2,3,1,0:T(8,128)S(1)} %convolution_subtract_fusion.1, f32[2,32,64,64]{2,3,1,0:T(8,128)S(1)} %convolution_add_fusion.1, f32[64,64]{0,1:T(8,128)S(1)} %copy.175, f32[64,64]{0,1:T(8,128)S(1)} %copy.174), kind=kOutput, calls=%fused_computation.71 | convolution fusion | flops 101478400 | bytes 2654208 | tf_op jit(solution)/shard_map/nk,...km->...nm/dot_general | solution.py:37
  354.1 7.7 %fusion.22 = f32[2,32,32,64]{3,2,1,0:T(8,128)S(1)} fusion(f32[2,32,64,32]{2,3,1,0:T(8,128)} %fusion.35, f32[2,32,64,64]{2,3,1,0:T(8,128)S(1)} %convolution_add_fusion.1, f32[2,32,64,64]{2,3,1,0:T(8,128)} %copy-done.3, f32[64,64]{0,1:T(8,128)S(1)} %copy.175, f32[64,64]{0,1:T(8,128)S(1)} %copy.174), kind=kOutput, calls=%fused_computation.58 | convolution fusion | flops 101609472 | bytes 3178496 | tf_op jit(solution)/shard_map/nk,...km->...nm/dot_general | solution.py:37
  364.1 28.5 %gather_fusion.5 = f32[4096,2,32]{2,1,0:T(2,128)} fusion(f32[2,2048,32]{2,0,1:T(2,128)S(1)} %bitcast.228, s32[4096]{0:T(1024)S(1)} %broadcast_clamp_fusion), kind=kCustom, calls=%fused_computation.1.clone | custom fusion | bytes 2113536 | tf_op jit(solution)/shard_map/jit(_take)/gather | solution.py:131
  392.6 30.1 %gather_fusion.6 = f32[4096,2,32]{2,1,0:T(2,128)} fusion(f32[2,2048,32]{2,0,1:T(2,128)} %bitcast.229, s32[4096]{0:T(1024)S(1)} %broadcast_clamp_fusion), kind=kCustom, calls=%fused_computation.3.clone | custom fusion | bytes 2113536 | tf_op jit(solution)/shard_map/jit(_take)/gather | solution.py:131
  422.8 22.9 %bitcast_select_fusion = (f32[2,4096,32]{2,0,1:T(2,128)}, f32[2,4096,32]{2,0,1:T(2,128)}) fusion(f32[4096,2,32]{2,1,0:T(2,128)} %gather_fusion.6, pred[4096]{0:T(1024)(128)(4,1)S(1)} %get-tuple-element.17, pred[4096]{0:T(1024)(128)(4,1)S(1)} %get-tuple-element.18, f32[4096,2,32]{2,1,0:T(2,128)} %gather_fusion.5), kind=kLoop, calls=%fused_computation.8 | loop fusion | flops 1048576 | bytes 4202496 | tf_op jit(solution)/shard_map/jit(_where)/select_n | solution.py:131
  445.6 6.9 %reshape.336 = f32[128,1,2048]{2,1,0:T(1,128)} reshape(f32[4096,2,32]{2,1,0:T(2,128)} %bitcast.241) | data formatting | bytes 2097152
  452.5 10.2 %all-to-all-start.3 = ((f32[128,1,2048]{2,1,0:T(1,128)}), f32[128,1,2048]{2,1,0:T(1,128)}, u32[]{:S(2)}, u32[]{:S(2)}) async-start(f32[128,1,2048]{2,1,0:T(1,128)} %reshape.336), calls=%async_computation.3 | async-start | bytes 2097152 | tf_op jit(solution)/shard_map/all_to_all | solution.py:148
  478.1 6.5 %reshape.334 = f32[128,1,2048]{2,1,0:T(1,128)} reshape(f32[4096,2,32]{2,1,0:T(2,128)} %bitcast.240) | data formatting | bytes 2097152
  484.6 14.5 %all-to-all-start.2 = ((f32[128,1,2048]{2,1,0:T(1,128)}), f32[128,1,2048]{2,1,0:T(1,128)}, u32[]{:S(2)}, u32[]{:S(2)}) async-start(f32[128,1,2048]{2,1,0:T(1,128)} %reshape.334), calls=%async_computation.2 | async-start | bytes 2097152 | tf_op jit(solution)/shard_map/all_to_all | solution.py:147
  520.6 6.6 %copy.284 = f32[2,128,32,32]{3,1,2,0:T(8,128)} copy(f32[2,128,32,32]{3,0,2,1:T(2,128)} %bitcast.234) | data formatting | bytes 2097152 | tf_op jit(solution)/shard_map/all_to_all | solution.py:148
  543.4 6.6 %copy.285 = f32[2,128,32,32]{3,1,2,0:T(8,128)} copy(f32[2,128,32,32]{3,0,2,1:T(2,128)} %bitcast.235) | data formatting | bytes 2097152 | tf_op jit(solution)/shard_map/all_to_all | solution.py:147
  (132 shorter events, 212.3 us)
Async XLA Ops:
  0.0 503.5 %copy-start = (bf16[384,384]{1,0:T(8,128)(2,1)S(1)}, bf16[384,384]{1,0:T(8,128)(2,1)}, u32[]{:S(2)}) copy-start(bf16[384,384]{1,0:T(8,128)(2,1)} %param.12) | copy-start | bytes 884740
  0.0 2.1 slice-start
  2.1 0.6 copy-start.19
  21.6 5.5 copy-start.2
  45.9 107.3 %all-to-all-start = ((f32[128,1,2048]{2,1,0:T(1,128)}), f32[128,1,2048]{2,1,0:T(1,128)}, u32[]{:S(2)}, u32[]{:S(2)}) async-start(f32[128,1,2048]{2,1,0:T(1,128)} %reshape.330), calls=%async_computation | async-start | bytes 2097152 | tf_op jit(solution)/shard_map/all_to_all | solution.py:135
  57.9 6.6 %copy-start.1 = (s32[128]{0:T(128)S(1)}, s32[128]{0:T(128)}, u32[]{:S(2)}) copy-start(s32[128]{0:T(128)} %param.16) | copy-start | bytes 1540
  153.2 48.5 %all-to-all-start.1 = ((f32[128,1,2048]{2,1,0:T(1,128)}), f32[128,1,2048]{2,1,0:T(1,128)S(1)}, u32[]{:S(2)}, u32[]{:S(2)}) async-start(f32[128,1,2048]{2,1,0:T(1,128)} %reshape.332), calls=%async_computation.1 | async-start | bytes 2097152 | tf_op jit(solution)/shard_map/all_to_all | solution.py:136
  163.0 12.6 %copy-start.14 = (f32[32,4096]{1,0:T(8,128)S(1)}, f32[32,4096]{1,0:T(8,128)}, u32[]{:S(2)}) copy-start(f32[32,4096]{1,0:T(8,128)} %param.17) | copy-start | bytes 1572868
  240.9 16.7 %copy-start.15 = (pred[2048]{0:T(1024)(128)(4,1)S(1)}, pred[2048]{0:T(1024)(128)(4,1)}, u32[]{:S(2)}) copy-start(pred[2048]{0:T(1024)(128)(4,1)} %get-tuple-element.6) | copy-start | bytes 6148
  284.1 5.3 copy-start.12
  332.9 12.9 %copy-start.3 = (f32[2,32,64,64]{2,3,1,0:T(8,128)}, f32[2,32,64,64]{2,3,1,0:T(8,128)S(1)}, u32[]{:S(2)}) copy-start(f32[2,32,64,64]{2,3,1,0:T(8,128)S(1)} %convolution_subtract_fusion.1) | copy-start | bytes 3145732
  361.8 2.4 copy-start.6
  445.6 17.1 %copy-start.4 = (f32[4,256,2,384]{3,2,1,0:T(2,128)S(1)}, f32[4,256,2,384]{3,2,1,0:T(2,128)}, u32[]{:S(2)}) copy-start(f32[4,256,2,384]{3,2,1,0:T(2,128)} %param.11) | copy-start | bytes 9437188
  452.5 32.1 %all-to-all-start.3 = ((f32[128,1,2048]{2,1,0:T(1,128)}), f32[128,1,2048]{2,1,0:T(1,128)}, u32[]{:S(2)}, u32[]{:S(2)}) async-start(f32[128,1,2048]{2,1,0:T(1,128)} %reshape.336), calls=%async_computation.3 | async-start | bytes 2097152 | tf_op jit(solution)/shard_map/all_to_all | solution.py:148
  463.9 10.2 %copy-start.16 = (s32[4,256]{1,0:T(4,128)S(1)}, s32[4,256]{1,0:T(4,128)}, u32[]{:S(2)}) copy-start(s32[4,256]{1,0:T(4,128)} %param.15) | copy-start | bytes 12292
  463.9 10.2 %copy-start.17 = (f32[384]{0:T(512)S(1)}, f32[384]{0:T(512)}, u32[]{:S(2)}) copy-start(f32[384]{0:T(512)} %param.14) | copy-start | bytes 4612
  463.9 38.3 %collective-permute-start.1 = (f32[1,256,2,384]{3,2,1,0:T(2,128)}, f32[1,256,2,384]{3,2,1,0:T(2,128)}, u32[]{:S(2)}, u32[]{:S(2)}) collective-permute-start(f32[1,256,2,384]{3,2,1,0:T(2,128)} %slice.25), channel_id=1, source_target_pairs={{1,0},{2,1},{3,2},{4,3},{5,4},{6,5},{7,6},{8,7},{9,8},{10,9},{11,1... | collective-permute-start | bytes 2359304 | tf_op jit(solution)/shard_map/ppermute | solution.py:21
  471.6 31.9 %collective-permute-start = (f32[1,256,2,384]{3,1,2,0:T(8,128)}, f32[1,256,2,384]{3,1,2,0:T(8,128)}, u32[]{:S(2)}, u32[]{:S(2)}) collective-permute-start(f32[1,256,2,384]{3,1,2,0:T(8,128)} %constant_dynamic-slice_fusion), channel_id=1, source_target_pairs={{0,1},{1,2},{2,3},{3,4},{4,5},{5,6},{6,7},{7,8},{8,9},{9,10},{10,1... | collective-permute-start | bytes 2359304 | tf_op jit(solution)/shard_map/ppermute | solution.py:20
  484.6 49.5 %all-to-all-start.2 = ((f32[128,1,2048]{2,1,0:T(1,128)}), f32[128,1,2048]{2,1,0:T(1,128)}, u32[]{:S(2)}, u32[]{:S(2)}) async-start(f32[128,1,2048]{2,1,0:T(1,128)} %reshape.334), calls=%async_computation.2 | async-start | bytes 2097152 | tf_op jit(solution)/shard_map/all_to_all | solution.py:147
  499.1 4.4 copy-start.9
  499.1 4.4 copy-start.10
  499.1 4.4 copy-start.13
  499.1 4.4 copy-start.18
  507.0 1.7 copy-start.7
  554.8 3.9 copy-start.5
  554.8 3.9 copy-start.11
  585.5 4.2 copy-start.8
  585.5 4.2 copy-start.20
where the time goes:
time: 607 us; the launch traced here: 595 us
  local copies, waits for them, and re-layouts  335 us (55%)
  matrix products  145 us (24%)
  other arithmetic  60.8 us (10%)
  starting transfers between devices  52.1 us (9%)
    dot_general x28, matrix products, apply_left(): return jnp.einsum(pattern, matrix, values, precision=lax.Precision.HIGHEST)  141 us
    gather x2, local copies, waits for them, and re-layouts, expand(): jnp.take(values, grid_of_slot, axis=1)  58.6 us
    unnamed x52, local copies, waits for them, and re-layouts  50.8 us
    gather x1, local copies, waits for them, and re-layouts, per_device(): slot_used = slot_place < row_counts[slot_device]  42.4 us
    gather x2, local copies, waits for them, and re-layouts, compact(): return jnp.take(values, gather_rows, axis=1)  33.4 us
    gather x1, local copies, waits for them, and re-layouts, per_device(): starts[slot_device] + slot_place  24.7 us
    select_n x1, other arithmetic, expand(): jnp.where(slot_used[None, :, None], jnp.take(values, grid_of_slot, axis=1...  22.9 us
    all_to_all x3, local copies, waits for them, and re-layouts, per_device(): lax.all_to_all(imag_part, 'row', split_axis=2, concat_axis=1, tiled=True)  14.7 us
  transfers between devices with their start and end apart: 6, of which 0 were waited for; matrix products, arithmetic and copies ran while one was open for 31% of the time, Pallas kernels for 0%

commit v1 on v0

v1 whole, which is shorter than its diff:
```python
import math

import jax
import jax.numpy as jnp
import numpy as np
from jax import lax
from jax.experimental import pallas as pl
from jax.experimental.pallas import tpu as pltpu
from jax.sharding import PartitionSpec as P

CELL = 8
HALF = 512
CELLS = 256
PAD = 4096
SLOTS = 4
DEVICES = 128
VMEM_LIMIT = 48 * 1024 * 1024
F32 = jnp.float32
BF16 = jnp.bfloat16


def hi_lo_constant(values):
    values = np.asarray(values, np.float32)
    high = values.astype(jnp.bfloat16)
    low = (values - high.astype(np.float32)).astype(jnp.bfloat16)
    return np.stack([high, low])


def dft_table():
    cell = np.arange(CELLS)[:, None]
    freq = np.arange(HALF)[None, :]
    phase = (cell * freq % HALF) * (2.0 * math.pi / HALF)
    return hi_lo_constant(np.concatenate([np.cos(phase), np.sin(phase)], axis=0))


def twiddle_table():
    point = np.arange(CELL)[:, None]
    freq = np.arange(HALF)[None, :]
    phase = point * freq * (2.0 * math.pi / PAD)
    return np.concatenate([np.cos(phase), np.sin(phase)], axis=0).astype(np.float32)


def dof_order_table(scale):
    table = np.zeros((CELL, CELL, SLOTS, SLOTS, 128), np.float32)
    for b in range(CELL):
        for a in range(CELL):
            for slot in range(SLOTS):
                table[b, a, slot, slot, a * CELL + b] = scale
    return table.reshape(CELL * CELL * SLOTS, SLOTS * 128).astype(jnp.bfloat16)


def split(values):
    high = values.astype(BF16)
    return high, (values - high.astype(F32)).astype(BF16)


def dot(left, right):
    return jnp.dot(left, right, preferred_element_type=F32)


def dot_nt(left, right):
    return lax.dot_general(left, right, (((1,), (1,)), ((), ())), preferred_element_type=F32)


def dot3(left, right_ref):
    high, low = split(left)
    return dot(high, right_ref[0]) + (dot(high, right_ref[1]) + dot(low, right_ref[0]))


def dot3_nt(left_high, left_low, right):
    high, low = split(right)
    return dot_nt(left_high, high) + (dot_nt(left_high, low) + dot_nt(left_low, high))


ROOT = math.sqrt(0.5)


def cadd(x, y):
    return (x[0] + y[0], x[1] + y[1])


def csub(x, y):
    return (x[0] - y[0], x[1] - y[1])


def turn(x, eighths, sign):
    re, im = x
    if eighths == 0:
        return x
    if eighths == 2:
        return (-im, re) if sign > 0 else (im, -re)
    if eighths == 1:
        return ((re - im) * ROOT, (im + re) * ROOT) if sign > 0 else ((re + im) * ROOT, (im - re) * ROOT)
    return ((-re - im) * ROOT, (re - im) * ROOT) if sign > 0 else ((im - re) * ROOT, (-re - im) * ROOT)


def dft4(x, sign):
    s0, d0 = cadd(x[0], x[2]), csub(x[0], x[2])
    s1, d1 = cadd(x[1], x[3]), turn(csub(x[1], x[3]), 2, sign)
    return [cadd(s0, s1), cadd(d0, d1), csub(s0, s1), csub(d0, d1)]


def dft8(x, sign):
    even = dft4([cadd(x[n], x[n + 4]) for n in range(4)], sign)
    odd = dft4([turn(csub(x[n], x[n + 4]), n, sign) for n in range(4)], sign)
    return [v for pair in zip(even, odd) for v in pair]


def twist(x, cos, sin, sign):
    re, im = x
    if sign > 0:
        return (re * cos - im * sin, im * cos + re * sin)
    return (re * cos + im * sin, im * cos - re * sin)


def swap_groups(tiles, lane):
    low_half = lane < 64
    t0, t1, t2, t3 = tiles
    u0 = jnp.where(low_half, t0, pltpu.roll(t2, 64, 1))
    u2 = jnp.where(low_half, pltpu.roll(t0, 64, 1), t2)
    u1 = jnp.where(low_half, t1, pltpu.roll(t3, 64, 1))
    u3 = jnp.where(low_half, pltpu.roll(t1, 64, 1), t3)
    even = lax.rem(lane, 64) < 32
    return [
        jnp.where(even, u0, pltpu.roll(u1, 32, 1)),
        jnp.where(even, pltpu.roll(u0, 96, 1), u1),
        jnp.where(even, u2, pltpu.roll(u3, 32, 1)),
        jnp.where(even, pltpu.roll(u2, 96, 1), u3),
    ]


def tile(ref, part, block, row, lane_tile):
    start = part * 256 + block * 32 + row * 8
    return ref.at[start:start + 8, lane_tile * 128:lane_tile * 128 + 128]


def forward_kernel(x_ref, order_ref, table_ref, twist_ref, out_ref, y_ref):
    planes = []
    for c in range(2):
        plane = jnp.concatenate([x_ref[slot, :, c, :] for slot in range(SLOTS)], axis=1)
        high, low = split(plane)
        planes.append(dot_nt(order_ref[...], high) + dot_nt(order_ref[...], low))
    w0, w1 = planes
    stacked = jnp.concatenate(
        [jnp.concatenate([w0, w1], axis=1), jnp.concatenate([w1, -w0], axis=1)], axis=0
    )
    y_ref[...] = dot3(stacked, table_ref)
    lane = lax.broadcasted_iota(jnp.int32, (8, 128), 1)
    for lane_tile in range(4):
        cut = slice(lane_tile * 128, lane_tile * 128 + 128)
        for row in range(4):
            points = []
            for b in range(CELL):
                value = tuple(tile(y_ref, o, b, row, lane_tile)[...] for o in range(2))
                if b:
                    value = twist(value, twist_ref[b:b + 1, cut], twist_ref[8 + b:9 + b, cut], -1)
                points.append(value)
            for k, value in enumerate(dft8(points, -1)):
                for o in range(2):
                    tile(y_ref, o, k, row, lane_tile)[...] = value[o]
        for k in range(CELL):
            for o in range(2):
                tiles = [tile(y_ref, o, k, row, lane_tile)[...] for row in range(4)]
                for u, value in enumerate(swap_groups(tiles, lane)):
                    out_ref[k * 16 + lane_tile * 4 + u, o * 8:o * 8 + 8, :] = value


def middle_kernel(x_ref, across_ref, down_ref, table_ref, twist_ref, green_ref, out_ref, y_ref):
    rows = jnp.concatenate(
        [x_ref[:, c * 8:c * 8 + 8, :].reshape(1024, 128) for c in range(2)], axis=1
    )
    high, low = split(rows)
    place = lax.broadcasted_iota(jnp.int32, (512, 1024), 0)
    chosen = jnp.where(place == across_ref[...], 1.0, 0.0).astype(BF16)
    compact = dot(chosen, high) + dot(chosen, low)
    w = [
        jnp.concatenate(
            [compact[h * 256:h * 256 + 256, c * 128:c * 128 + 128].T for h in range(2)], axis=0
        )
        for c in range(2)
    ]
    stacked = jnp.concatenate(
        [jnp.concatenate([w[0], w[1]], axis=1), jnp.concatenate([w[1], -w[0]], axis=1)], axis=0
    )
    y_ref[...] = dot3(stacked, table_ref)
    for lane_tile in range(4):
        cut = slice(lane_tile * 128, lane_tile * 128 + 128)
        for row in range(4):
            points = []
            for a in range(CELL):
                block = (a % 2) * 4 + a // 2
                value = tuple(tile(y_ref, o, block, row, lane_tile)[...] for o in range(2))
                if a:
                    value = twist(value, twist_ref[a:a + 1, cut], twist_ref[8 + a:9 + a, cut], -1)
                points.append(value)
            spectrum = []
            for q, value in enumerate(dft8(points, -1)):
                first = q * 512 + lane_tile * 128
                green = green_ref[row * 8:row * 8 + 8, first:first + 128]
                spectrum.append((value[0] * green, value[1] * green))
            for a, value in enumerate(dft8(spectrum, 1)):
                block = (a % 2) * 4 + a // 2
                if a:
                    value = twist(value, twist_ref[a:a + 1, cut], twist_ref[8 + a:9 + a, cut], 1)
                for o in range(2):
                    tile(y_ref, o, block, row, lane_tile)[...] = value[o]
    back = inverse_cells(y_ref, table_ref)
    pieces = [
        jnp.concatenate(
            [back[:, c * 256 + h * 128:c * 256 + h * 128 + 128] for c in range(2)], axis=1
        )
        for h in range(2)
    ]
    high, low = split(jnp.concatenate(pieces, axis=0))
    place = lax.broadcasted_iota(jnp.int32, (1024, 128), 1)
    down = down_ref[...]
    spread = jnp.concatenate(
        [jnp.where(place + 128 * n == down, 1.0, 0.0).astype(BF16) for n in range(4)], axis=1
    )
    result = dot(spread, high) + dot(spread, low)
    for c in range(2):
        out_ref[:, c * 8:c * 8 + 8, :] = result[:, c * 128:c * 128 + 128].reshape(128, 8, 128)


def inverse_cells(y_ref, table_ref):
    re, im = y_ref[0:256, :], y_ref[256:512, :]
    by_cos = jnp.concatenate([re, im], axis=0)
    by_sin = jnp.concatenate([-im, re], axis=0)
    return dot3_nt(table_ref[0, 0:256, :], table_ref[1, 0:256, :], by_cos) + dot3_nt(
        table_ref[0, 256:512, :], table_ref[1, 256:512, :], by_sin
    )


def backward_kernel(x_ref, part_ref, order_ref, table_ref, twist_ref, out_ref, y_ref):
    lane = lax.broadcasted_iota(jnp.int32, (8, 128), 1)
    for lane_tile in range(4):
        cut = slice(lane_tile * 128, lane_tile * 128 + 128)
        for k in range(CELL):
            for o in range(2):
                tiles = [x_ref[k * 16 + lane_tile * 4 + u, o * 8:o * 8 + 8, :] for u in range(4)]
                for row, value in enumerate(swap_groups(tiles, lane)):
                    tile(y_ref, o, k, row, lane_tile)[...] = value
        for row in range(4):
            points = [
                tuple(tile(y_ref, o, k, row, lane_tile)[...] for o in range(2))
                for k in range(CELL)
            ]
            for b, value in enumerate(dft8(points, 1)):
                if b:
                    value = twist(value, twist_ref[b:b + 1, cut], twist_ref[8 + b:9 + b, cut], 1)
                for o in range(2):
                    tile(y_ref, o, b, row, lane_tile)[...] = value[o]
    back = inverse_cells(y_ref, table_ref)
    for c in range(2):
        high, low = split(back[:, c * 256:c * 256 + 256])
        plane = dot(high, order_ref[...]) + dot(low, order_ref[...])
        for slot in range(SLOTS):
            out_ref[slot, :, c, :] = (
                part_ref[slot, :, c, :] + plane[:, slot * 128:slot * 128 + 128]
            )


def structural_kernel(
    count_ref, x_ref, above_ref, below_ref, stiff_ref, couple_ref, soft_ref, mask_ref, out_ref
):
    count = count_ref[0]
    cell = lax.broadcasted_iota(jnp.int32, (CELLS, 1), 0)
    for slot in range(SLOTS):
        biased = mask_ref[:, slot:slot + 1]
        used = slot < count
        last = slot == count - 1
        for c in range(2):
            own = x_ref[slot, :, c, :]
            elastic = dot(own.astype(BF16), stiff_ref[...])
            before = above_ref[:, c, :] if slot == 0 else x_ref[slot - 1, :, c, :]
            after = below_ref[:, c, :]
            if slot < SLOTS - 1:
                after = jnp.where(last, after, x_ref[slot + 1, :, c, :])
            left = jnp.where(cell == 0, 0.0, pltpu.roll(own, 1, 0))
            right = jnp.where(cell == CELLS - 1, 0.0, pltpu.roll(own, CELLS - 1, 0))
            beside = before + after + left + right
            value = elastic - couple_ref[...] * beside - (biased * soft_ref[...]) * own
            out_ref[slot, :, c, :] = jnp.where(used, value, 0.0)


def whole(*shape):
    return pl.BlockSpec(shape, lambda i: (0,) * len(shape))


def per_device(
    displacement, stiffness, coupling, softening, electrode_mask, row_counts, green_spectrum
):
    devices = lax.axis_size("row")
    position = lax.axis_index("row")
    table = jnp.asarray(dft_table())
    turns = jnp.asarray(twiddle_table())
    params = pltpu.CompilerParams(vmem_limit_bytes=VMEM_LIMIT)
    surface_block = pl.BlockSpec((SLOTS, CELLS, 2, 128), lambda i: (0, 0, 0, 0))
    own_count = row_counts[position]
    up = [(i, i + 1) for i in range(devices - 1)]
    down = [(j, i) for i, j in up]
    last_used = lax.dynamic_slice_in_dim(displacement, own_count - 1, 1, 0)
    above = lax.ppermute(last_used, "row", up)
    below = lax.ppermute(displacement[:1], "row", down)

    sent = pl.pallas_call(
        forward_kernel,
        grid=(1,),
        in_specs=[surface_block, whole(256, 512), whole(2, 512, 512), whole(16, 512)],
        out_specs=whole(DEVICES, 16, 128),
        out_shape=jax.ShapeDtypeStruct((DEVICES, 16, 128), F32),
        scratch_shapes=[pltpu.VMEM((512, 512), F32)],
        compiler_params=params,
        cost_estimate=pl.CostEstimate(flops=10**9, bytes_accessed=4 << 20, transcendentals=0),
    )(displacement, jnp.asarray(dof_order_table(1.0)), table, turns)
    received = lax.all_to_all(sent, "row", split_axis=0, concat_axis=0, tiled=True)

    before = jnp.arange(DEVICES)[:, None] > jnp.arange(DEVICES)[None, :]
    starts = jnp.sum(jnp.where(before, row_counts[None, :], 0), axis=1)
    half = jnp.arange(2, dtype=jnp.int32)[None, :, None]
    slot = jnp.arange(SLOTS, dtype=jnp.int32)[None, None, :]
    cell_row = starts[:, None, None] + slot
    place = jnp.where(slot < row_counts[:, None, None], half * CELLS + cell_row, -1)
    place = place.reshape(1024).astype(jnp.int32)
    across = place.reshape(1, 1024)
    downward = jnp.broadcast_to(place[:, None], (1024, 128))

    sent = pl.pallas_call(
        middle_kernel,
        grid=(1,),
        in_specs=[
            whole(DEVICES, 16, 128), whole(1, 1024), whole(1024, 128),
            whole(2, 512, 512), whole(16, 512), whole(32, PAD),
        ],
        out_specs=whole(DEVICES, 16, 128),
        out_shape=jax.ShapeDtypeStruct((DEVICES, 16, 128), F32),
        scratch_shapes=[pltpu.VMEM((512, 512), F32)],
        compiler_params=params,
        cost_estimate=pl.CostEstimate(flops=3 * 10**9, bytes_accessed=5 << 20, transcendentals=0),
    )(received, across, downward, table, turns, green_spectrum)
    received = lax.all_to_all(sent, "row", split_axis=0, concat_axis=0, tiled=True)

    full_block = whole(SLOTS, CELLS, 2, 384)
    structural = pl.pallas_call(
        structural_kernel,
        grid=(1,),
        in_specs=[
            pl.BlockSpec(memory_space=pltpu.SMEM),
            full_block, whole(CELLS, 2, 384), whole(CELLS, 2, 384), whole(384, 384),
            whole(1, 384), whole(1, 384), whole(CELLS, SLOTS),
        ],
        out_specs=full_block,
        out_shape=jax.ShapeDtypeStruct(displacement.shape, F32),
        compiler_params=params,
        cost_estimate=pl.CostEstimate(flops=10**9, bytes_accessed=8 << 20, transcendentals=0),
    )(
        own_count.reshape(1), displacement, above[0], below[0], stiffness,
        coupling[None, :], softening[None, :], electrode_mask.astype(F32).T,
    )
    return pl.pallas_call(
        backward_kernel,
        grid=(1,),
        in_specs=[
            whole(DEVICES, 16, 128), surface_block, whole(256, 512),
            whole(2, 512, 512), whole(16, 512),
        ],
        out_specs=surface_block,
        out_shape=jax.ShapeDtypeStruct(displacement.shape, F32),
        scratch_shapes=[pltpu.VMEM((512, 512), F32)],
        input_output_aliases={1: 0},
        compiler_params=params,
        cost_estimate=pl.CostEstimate(flops=10**9, bytes_accessed=4 << 20, transcendentals=0),
    )(received, structural, jnp.asarray(dof_order_table(1.0 / (PAD * PAD))), table, turns)


def solution(mesh):
    placed = (P("row", None, None, None), P(), P(), P(), P("row", None), P(), P("row", None))
    return jax.shard_map(
        per_device,
        mesh=mesh,
        in_specs=placed,
        out_specs=P("row", None, None, None),
        check_vma=False,
    )
```

time: 607 us -> 104 us (0.17)
  the two profiles are of different devices: /device:TPU:1 before, /device:TPU:24 now
where the time goes in v1:
time: 104 us; the launch traced here: 103 us
  waiting for transfers between devices  30.8 us (30%)
  Pallas kernels  26.9 us (26%)
  starting transfers between devices  26.8 us (26%)
  local copies, waits for them, and re-layouts  16.3 us (16%)
  between operations  1.56 us (2%)
    all_to_all x2, starting transfers between devices, per_device(): lax.all_to_all(sent, 'row', split_axis=0, concat_axis=0, tiled=True)  17.2 us
    all_to_all x2, waiting for transfers between devices, per_device(): lax.all_to_all(sent, 'row', split_axis=0, concat_axis=0, tiled=True)  15.3 us
    unnamed x38, local copies, waits for them, and re-layouts  13.2 us
    pallas_call x1, Pallas kernels, per_device(): pl.pallas_call(structural_kernel, grid=(1,), in_specs=[pl.BlockSpec(memor...  11.5 us
    ppermute x1, waiting for transfers between devices, per_device(): below = lax.ppermute(displacement[:1], 'row', down)  8.2 us
    ppermute x1, starting transfers between devices, per_device(): below = lax.ppermute(displacement[:1], 'row', down)  7.52 us
    ppermute x1, waiting for transfers between devices, per_device(): above = lax.ppermute(last_used, 'row', up)  7.33 us
    pallas_call x1, Pallas kernels, per_device(): pl.pallas_call(middle_kernel, grid=(1,), in_specs=[whole(DEVICES, 16, 128...  6.12 us
  transfers between devices with their start and end apart: 4, of which 3 were waited for; matrix products, arithmetic and copies ran while one was open for 3% of the time, Pallas kernels for 11%

profile of v1, /device:TPU:24, one launch (start us, length us, event | category | flops | bytes accessed | tf_op | source)
XLA Modules:
  0.0 102.9 jit_solution(6146922399164217514)
XLA Ops:
  0.0 1.9 %copy-done = f32[4,256,2,384]{3,2,1,0:T(2,128)S(1)} copy-done((f32[4,256,2,384]{3,2,1,0:T(2,128)S(1)}, f32[4,256,2,384]{3,2,1,0:T(2,128)}, u32[]{:S(2)}) %copy-start) | copy-done | bytes 3145752
  1.9 1.2 %copy-done.2 = bf16[2,512,512]{2,1,0:T(8,128)(2,1)S(1)} copy-done((bf16[2,512,512]{2,1,0:T(8,128)(2,1)S(1)}, bf16[2,512,512]{2,1,0:T(8,128)(2,1)}, u32[]{:S(2)}) %copy-start.2) | copy-done | bytes 1048600
  3.1 0.9 copy-done.10
  4.1 0.8 copy-done.11
  4.8 3.9 %shard_map.109 = f32[128,16,128]{2,1,0:T(8,128)} custom-call(f32[4,256,2,384]{3,2,1,0:T(2,128)S(1)} %copy-done, bf16[256,512]{1,0:T(8,128)(2,1)S(1)} %copy-done.10, bf16[2,512,512]{2,1,0:T(8,128)(2,1)S(1)} %copy-done.2, f32[16,512]{1,0:T(8,128)S(1)} %copy-done.11), custom_call_target="tpu_custom_call" | custom-call | flops 1000000000 | bytes 4194304 | tf_op jit(solution)/shard_map/pallas_call | solution.py:306
  8.8 10.3 %all-to-all-start = ((f32[128,16,128]{2,1,0:T(8,128)}), f32[128,16,128]{2,1,0:T(8,128)S(1)}, u32[]{:S(2)}, u32[]{:S(2)}) async-start(f32[128,16,128]{2,1,0:T(8,128)} %shard_map.109), calls=%async_computation | async-start | bytes 2097152 | tf_op jit(solution)/shard_map/all_to_all | solution.py:316
  19.1 0.1 select_reduce_fusion
  19.2 0.1 iota_compare_fusion.1
  19.4 0.1 add_select_fusion
  19.5 0.2 select_n.34
  19.7 0.2 select_n.33.across_ref
  19.9 0.7 dynamic_slice.6.count_ref
  21.9 15.3 %all-to-all-done.x_ref = f32[128,16,128]{2,1,0:T(8,128)S(1)} async-done(((f32[128,16,128]{2,1,0:T(8,128)}), f32[128,16,128]{2,1,0:T(8,128)S(1)}, u32[]{:S(2)}, u32[]{:S(2)}) %all-to-all-start) | async-done | bytes 1048608 | tf_op jit(solution)/shard_map/all_to_all | solution.py:316
  37.2 1.0 copy-done.5
  38.2 0.2 broadcast_in_dim.46.down_ref
  38.4 1.2 %copy-done.3 = bf16[2,512,512]{2,1,0:T(8,128)(2,1)S(1)} copy-done((bf16[2,512,512]{2,1,0:T(8,128)(2,1)S(1)}, bf16[2,512,512]{2,1,0:T(8,128)(2,1)}, u32[]{:S(2)}) %copy-start.3) | copy-done | bytes 1048600
  39.6 1.2 %copy-done.6 = f32[128,16,128]{2,1,0:T(8,128)S(1)} copy-done((f32[128,16,128]{2,1,0:T(8,128)S(1)}, f32[128,16,128]{2,1,0:T(8,128)}, u32[]{:S(2)}) %copy-start.6) | copy-done | bytes 1048600
  40.9 1.0 %copy-done.14 = f32[32,4096]{1,0:T(8,128)S(1)} copy-done((f32[32,4096]{1,0:T(8,128)S(1)}, f32[32,4096]{1,0:T(8,128)}, u32[]{:S(2)}) %copy-start.14) | copy-done | bytes 524312
  41.9 6.1 %shard_map.110 = f32[128,16,128]{2,1,0:T(8,128)S(1)} custom-call(f32[128,16,128]{2,1,0:T(8,128)S(1)} %copy-done.6, s32[1,1024]{1,0:T(1,128)S(1)} %select_n.33.across_ref, s32[1024,128]{1,0:T(8,128)S(1)} %broadcast_in_dim.46.down_ref, bf16[2,512,512]{2,1,0:T(8,128)(2,1)S(1)} %copy-done.3, f32[16,512]{1,0:T(8,128)S(1)} %copy-done.12, f32[32,4096]{1,0:T(8,128)S(1)} %copy-done.14), custom_call_target="tpu_custom_call" | custom-call | flops 3000000000 | bytes 5242880 | tf_op jit(solution)/shard_map/pallas_call | solution.py:328
  48.0 1.0 copy-done.7
  49.0 6.9 %all-to-all-start.1 = ((f32[128,16,128]{2,1,0:T(8,128)}), f32[128,16,128]{2,1,0:T(8,128)}, u32[]{:S(2)}, u32[]{:S(2)}) async-start(f32[128,16,128]{2,1,0:T(8,128)} %copy-done.7), calls=%async_computation.1 | async-start | bytes 2097152 | tf_op jit(solution)/shard_map/all_to_all | solution.py:341
  56.0 1.7 %fusion = (f32[1,256,2,384]{3,2,1,0:T(2,128)}, f32[1,256,2,384]{3,2,1,0:T(2,128)}) fusion(f32[4,256,2,384]{3,2,1,0:T(2,128)S(1)} %copy-done.1, s32[]{:T(128)S(6)} %select_n.36), kind=kLoop, calls=%fused_computation.7 | loop fusion | bytes 3145732 | tf_op jit(solution)/shard_map/slice | solution.py:304
  57.7 7.5 %collective-permute-start.1 = (f32[1,256,2,384]{3,2,1,0:T(2,128)}, f32[1,256,2,384]{3,2,1,0:T(2,128)}, u32[]{:S(2)}, u32[]{:S(2)}) collective-permute-start(f32[1,256,2,384]{3,2,1,0:T(2,128)} %get-tuple-element.5), channel_id=1, source_target_pairs={{1,0},{2,1},{3,2},{4,3},{5,4},{6,5},{7,6},{8,7},{9,8},{10,9},{11,1... | collective-permute-start | bytes 2359304 | tf_op jit(solution)/shard_map/ppermute | solution.py:304
  65.2 2.1 %collective-permute-start = (f32[1,256,2,384]{3,2,1,0:T(2,128)}, f32[1,256,2,384]{3,2,1,0:T(2,128)}, u32[]{:S(2)}, u32[]{:S(2)}) collective-permute-start(f32[1,256,2,384]{3,2,1,0:T(2,128)} %get-tuple-element.6), channel_id=1, source_target_pairs={{0,1},{1,2},{2,3},{3,4},{4,5},{5,6},{6,7},{7,8},{8,9},{9,10},{10,1... | collective-permute-start | bytes 2359304 | tf_op jit(solution)/shard_map/ppermute | solution.py:303
  67.4 0.1 copy.15
  67.5 8.2 %collective-permute-done.1 = f32[1,256,2,384]{3,2,1,0:T(2,128)} collective-permute-done((f32[1,256,2,384]{3,2,1,0:T(2,128)}, f32[1,256,2,384]{3,2,1,0:T(2,128)}, u32[]{:S(2)}, u32[]{:S(2)}) %collective-permute-start.1) | collective-permute-done | bytes 786464 | tf_op jit(solution)/shard_map/ppermute | solution.py:304
  75.7 7.3 %collective-permute-done = f32[1,256,2,384]{3,2,1,0:T(2,128)} collective-permute-done((f32[1,256,2,384]{3,2,1,0:T(2,128)}, f32[1,256,2,384]{3,2,1,0:T(2,128)}, u32[]{:S(2)}, u32[]{:S(2)}) %collective-permute-start) | collective-permute-done | bytes 786464 | tf_op jit(solution)/shard_map/ppermute | solution.py:303
  83.0 1.0 copy-done.8
  84.0 11.5 %shard_map.111.part_ref = f32[4,256,2,384]{3,2,1,0:T(2,128)} custom-call(s32[1]{0:T(128)} %dynamic_slice.6.count_ref, f32[4,256,2,384]{3,2,1,0:T(2,128)S(1)} %copy-done.1, f32[256,2,384]{2,1,0:T(2,128)} %bitcast.2.above_ref, f32[256,2,384]{2,1,0:T(2,128)} %bitcast.3.below_ref, bf16[384,384]{1,0:T(8,128)(2,1)S(1)} %copy-done.8, ...), custom_call_target="tpu_custom_call" | custom-call | flops 1000000000 | bytes 8388608 | tf_op jit(solution)/shard_map/pallas_call | solution.py:344
  95.5 1.2 %copy-done.4 = bf16[2,512,512]{2,1,0:T(8,128)(2,1)S(1)} copy-done((bf16[2,512,512]{2,1,0:T(8,128)(2,1)S(1)}, bf16[2,512,512]{2,1,0:T(8,128)(2,1)}, u32[]{:S(2)}) %copy-start.4) | copy-done | bytes 1048600
  96.7 0.8 copy-done.13
  97.5 5.4 %shard_map.112 = f32[4,256,2,384]{3,2,1,0:T(2,128)} custom-call(f32[128,16,128]{2,1,0:T(8,128)} %all-to-all-done.1.x_ref, f32[4,256,2,384]{3,2,1,0:T(2,128)} %shard_map.111.part_ref, bf16[256,512]{1,0:T(8,128)(2,1)S(1)} %copy-done.9, bf16[2,512,512]{2,1,0:T(8,128)(2,1)S(1)} %copy-done.4, f32[16,512]{1,0:T(8,128)S(1)} %copy-done.13), custom_call_target="tpu_custom_call", output_to_operand_aliasing={{}: (1, {})} | custom-call | flops 1000000000 | bytes 4194304 | tf_op jit(solution)/shard_map/pallas_call | solution.py:360
  (32 shorter events, 0.1 us)
Async XLA Ops:
  0.0 1.9 %copy-start = (f32[4,256,2,384]{3,2,1,0:T(2,128)S(1)}, f32[4,256,2,384]{3,2,1,0:T(2,128)}, u32[]{:S(2)}) copy-start(f32[4,256,2,384]{3,2,1,0:T(2,128)} %x_ref.3) | copy-start | bytes 9437188
  1.9 1.2 %copy-start.2 = (bf16[2,512,512]{2,1,0:T(8,128)(2,1)S(1)}, bf16[2,512,512]{2,1,0:T(8,128)(2,1)}, u32[]{:S(2)}) copy-start(bf16[2,512,512]{2,1,0:T(8,128)(2,1)} %constant.28.clone.table_ref) | copy-start | bytes 3145732
  3.1 0.9 copy-start.10
  4.1 0.8 copy-start.11
  4.8 14.3 %copy-start.18 = (s32[128]{0:T(128)S(1)}, s32[128]{0:T(128)}, u32[]{:S(2)}) copy-start(s32[128]{0:T(128)} %param.16) | copy-start | bytes 1540
  4.8 33.6 %copy-start.12 = (f32[16,512]{1,0:T(8,128)S(1)}, f32[16,512]{1,0:T(8,128)}, u32[]{:S(2)}) copy-start(f32[16,512]{1,0:T(8,128)} %constant.29.clone.twist_ref) | copy-start | bytes 98308
  8.8 28.4 %all-to-all-start = ((f32[128,16,128]{2,1,0:T(8,128)}), f32[128,16,128]{2,1,0:T(8,128)S(1)}, u32[]{:S(2)}, u32[]{:S(2)}) async-start(f32[128,16,128]{2,1,0:T(8,128)} %shard_map.109), calls=%async_computation | async-start | bytes 2097152 | tf_op jit(solution)/shard_map/all_to_all | solution.py:316
  37.2 1.0 copy-start.5
  38.4 1.2 %copy-start.3 = (bf16[2,512,512]{2,1,0:T(8,128)(2,1)S(1)}, bf16[2,512,512]{2,1,0:T(8,128)(2,1)}, u32[]{:S(2)}) copy-start(bf16[2,512,512]{2,1,0:T(8,128)(2,1)} %constant.28.clone.table_ref) | copy-start | bytes 3145732
  39.6 1.2 %copy-start.6 = (f32[128,16,128]{2,1,0:T(8,128)S(1)}, f32[128,16,128]{2,1,0:T(8,128)}, u32[]{:S(2)}) copy-start(f32[128,16,128]{2,1,0:T(8,128)} %copy-done.5) | copy-start | bytes 3145732
  40.9 1.0 %copy-start.14 = (f32[32,4096]{1,0:T(8,128)S(1)}, f32[32,4096]{1,0:T(8,128)}, u32[]{:S(2)}) copy-start(f32[32,4096]{1,0:T(8,128)} %green_ref.1) | copy-start | bytes 1572868
  41.9 14.0 %copy-start.1 = (f32[4,256,2,384]{3,2,1,0:T(2,128)S(1)}, f32[4,256,2,384]{3,2,1,0:T(2,128)}, u32[]{:S(2)}) copy-start(f32[4,256,2,384]{3,2,1,0:T(2,128)} %x_ref.3) | copy-start | bytes 9437188
  48.0 1.0 copy-start.7
  49.0 18.3 %copy-start.16 = (f32[384]{0:T(512)S(1)}, f32[384]{0:T(512)}, u32[]{:S(2)}) copy-start(f32[384]{0:T(512)} %param.13) | copy-start | bytes 4612
  49.0 18.3 %copy-start.17 = (f32[384]{0:T(512)S(1)}, f32[384]{0:T(512)}, u32[]{:S(2)}) copy-start(f32[384]{0:T(512)} %param.14) | copy-start | bytes 4612
  49.0 18.3 %copy-start.15 = (s32[4,256]{1,0:T(4,128)S(1)}, s32[4,256]{1,0:T(4,128)}, u32[]{:S(2)}) copy-start(s32[4,256]{1,0:T(4,128)} %param.15) | copy-start | bytes 12292
  49.0 46.5 %all-to-all-start.1 = ((f32[128,16,128]{2,1,0:T(8,128)}), f32[128,16,128]{2,1,0:T(8,128)}, u32[]{:S(2)}, u32[]{:S(2)}) async-start(f32[128,16,128]{2,1,0:T(8,128)} %copy-done.7), calls=%async_computation.1 | async-start | bytes 2097152 | tf_op jit(solution)/shard_map/all_to_all | solution.py:341
  57.7 18.0 %collective-permute-start.1 = (f32[1,256,2,384]{3,2,1,0:T(2,128)}, f32[1,256,2,384]{3,2,1,0:T(2,128)}, u32[]{:S(2)}, u32[]{:S(2)}) collective-permute-start(f32[1,256,2,384]{3,2,1,0:T(2,128)} %get-tuple-element.5), channel_id=1, source_target_pairs={{1,0},{2,1},{3,2},{4,3},{5,4},{6,5},{7,6},{8,7},{9,8},{10,9},{11,1... | collective-permute-start | bytes 2359304 | tf_op jit(solution)/shard_map/ppermute | solution.py:304
  65.2 17.8 %collective-permute-start = (f32[1,256,2,384]{3,2,1,0:T(2,128)}, f32[1,256,2,384]{3,2,1,0:T(2,128)}, u32[]{:S(2)}, u32[]{:S(2)}) collective-permute-start(f32[1,256,2,384]{3,2,1,0:T(2,128)} %get-tuple-element.6), channel_id=1, source_target_pairs={{0,1},{1,2},{2,3},{3,4},{4,5},{5,6},{6,7},{7,8},{8,9},{9,10},{10,1... | collective-permute-start | bytes 2359304 | tf_op jit(solution)/shard_map/ppermute | solution.py:303
  83.0 1.0 copy-start.8
  84.0 11.5 %copy-start.9 = (bf16[256,512]{1,0:T(8,128)(2,1)S(1)}, bf16[256,512]{1,0:T(8,128)(2,1)}, u32[]{:S(2)}) copy-start(bf16[256,512]{1,0:T(8,128)(2,1)} %constant.31.clone.order_ref) | copy-start | bytes 786436
  95.5 1.2 %copy-start.4 = (bf16[2,512,512]{2,1,0:T(8,128)(2,1)S(1)}, bf16[2,512,512]{2,1,0:T(8,128)(2,1)}, u32[]{:S(2)}) copy-start(bf16[2,512,512]{2,1,0:T(8,128)(2,1)} %constant.28.clone.table_ref) | copy-start | bytes 3145732
  96.7 0.8 copy-start.13

commit v2 on v1

v2 whole, which is shorter than its diff:
```python
import math

import jax
import jax.numpy as jnp
import numpy as np
from jax import lax
from jax.experimental import pallas as pl
from jax.experimental.pallas import tpu as pltpu
from jax.sharding import PartitionSpec as P

CELL = 8
HALF = 512
CELLS = 256
PAD = 4096
SLOTS = 4
DEVICES = 128
VMEM_LIMIT = 60 * 1024 * 1024
F32 = jnp.float32
BF16 = jnp.bfloat16


def hi_lo_constant(values):
    values = np.asarray(values, np.float32)
    high = values.astype(jnp.bfloat16)
    low = (values - high.astype(np.float32)).astype(jnp.bfloat16)
    return np.stack([high, low])


def dft_table():
    cell = np.arange(CELLS)[:, None]
    freq = np.arange(HALF)[None, :]
    phase = (cell * freq % HALF) * (2.0 * math.pi / HALF)
    return hi_lo_constant(np.concatenate([np.cos(phase), np.sin(phase)], axis=0))


def twiddle_table():
    point = np.arange(CELL)[:, None]
    freq = np.arange(HALF)[None, :]
    phase = point * freq * (2.0 * math.pi / PAD)
    return np.concatenate([np.cos(phase), np.sin(phase)], axis=0).astype(np.float32)


def dof_order_table(scale):
    table = np.zeros((CELL, CELL // 2, SLOTS, 2, SLOTS, 128), np.float32)
    for b in range(CELL):
        for a in range(CELL):
            for slot in range(SLOTS):
                table[b, a // 2, slot, a % 2, slot, a * CELL + b] = scale
    return table.reshape(CELL * CELL * SLOTS, SLOTS * 128).astype(jnp.bfloat16)


def split(values):
    high = values.astype(BF16)
    return high, (values - high.astype(F32)).astype(BF16)


def dot(left, right):
    return jnp.dot(left, right, preferred_element_type=F32)


def dot_nt(left, right):
    return lax.dot_general(left, right, (((1,), (1,)), ((), ())), preferred_element_type=F32)


def dot3(left, right_ref):
    high, low = split(left)
    return dot(high, right_ref[0]) + (dot(high, right_ref[1]) + dot(low, right_ref[0]))


def dot3_nt(left_high, left_low, right):
    high, low = split(right)
    return dot_nt(left_high, high) + (dot_nt(left_high, low) + dot_nt(left_low, high))


ROOT = math.sqrt(0.5)


def cadd(x, y):
    return (x[0] + y[0], x[1] + y[1])


def csub(x, y):
    return (x[0] - y[0], x[1] - y[1])


def turn(x, eighths, sign):
    re, im = x
    if eighths == 0:
        return x
    if eighths == 2:
        return (-im, re) if sign > 0 else (im, -re)
    if eighths == 1:
        return ((re - im) * ROOT, (im + re) * ROOT) if sign > 0 else ((re + im) * ROOT, (im - re) * ROOT)
    return ((-re - im) * ROOT, (re - im) * ROOT) if sign > 0 else ((im - re) * ROOT, (-re - im) * ROOT)


def dft4(x, sign):
    s0, d0 = cadd(x[0], x[2]), csub(x[0], x[2])
    s1, d1 = cadd(x[1], x[3]), turn(csub(x[1], x[3]), 2, sign)
    return [cadd(s0, s1), cadd(d0, d1), csub(s0, s1), csub(d0, d1)]


def dft8(x, sign):
    even = dft4([cadd(x[n], x[n + 4]) for n in range(4)], sign)
    odd = dft4([turn(csub(x[n], x[n + 4]), n, sign) for n in range(4)], sign)
    return [v for pair in zip(even, odd) for v in pair]


def twist(x, cos, sin, sign):
    re, im = x
    if sign > 0:
        return (re * cos - im * sin, im * cos + re * sin)
    return (re * cos + im * sin, im * cos - re * sin)


def swap_groups(tiles, lane):
    low_half = lane < 64
    t0, t1, t2, t3 = tiles
    u0 = jnp.where(low_half, t0, pltpu.roll(t2, 64, 1))
    u2 = jnp.where(low_half, pltpu.roll(t0, 64, 1), t2)
    u1 = jnp.where(low_half, t1, pltpu.roll(t3, 64, 1))
    u3 = jnp.where(low_half, pltpu.roll(t1, 64, 1), t3)
    even = lax.rem(lane, 64) < 32
    return [
        jnp.where(even, u0, pltpu.roll(u1, 32, 1)),
        jnp.where(even, pltpu.roll(u0, 96, 1), u1),
        jnp.where(even, u2, pltpu.roll(u3, 32, 1)),
        jnp.where(even, pltpu.roll(u2, 96, 1), u3),
    ]


def tile(ref, part, block, row, lane_tile):
    start = part * 256 + block * 32 + row * 8
    return ref.at[start:start + 8, lane_tile * 128:lane_tile * 128 + 128]


def fetch(sources, targets, sems):
    copies = [
        pltpu.make_async_copy(source, target, sems.at[n])
        for n, (source, target) in enumerate(zip(sources, targets))
    ]
    for copy in copies:
        copy.start()
    return copies


def forward_kernel(
    x_hbm, order_hbm, table_hbm, twist_hbm, out_hbm,
    x_ref, order_ref, table_ref, twist_ref, out_ref, y_ref, sems, out_sems,
):
    copies = fetch(
        [x_hbm.at[slot] for slot in range(SLOTS)] + [order_hbm, table_hbm, twist_hbm],
        [x_ref.at[slot] for slot in range(SLOTS)] + [order_ref, table_ref, twist_ref],
        sems,
    )
    for copy in copies[:5]:
        copy.wait()
    planes = []
    for c in range(2):
        plane = jnp.concatenate([x_ref[slot, :, c, 0:128] for slot in range(SLOTS)], axis=1)
        high, low = split(plane)
        planes.append(dot_nt(order_ref[...], high) + dot_nt(order_ref[...], low))
    w0, w1 = planes
    stacked = jnp.concatenate(
        [jnp.concatenate([w0, w1], axis=1), jnp.concatenate([w1, -w0], axis=1)], axis=0
    )
    copies[5].wait()
    y_ref[...] = dot3(stacked, table_ref)
    copies[6].wait()
    lane = lax.broadcasted_iota(jnp.int32, (64, 128), 1)
    outs = []
    for lane_tile in range(4):
        cut = slice(lane_tile * 128, lane_tile * 128 + 128)
        for row in range(4):
            points = []
            for b in range(CELL):
                value = tuple(tile(y_ref, o, b, row, lane_tile)[...] for o in range(2))
                if b:
                    value = twist(value, twist_ref[b:b + 1, cut], twist_ref[8 + b:9 + b, cut], -1)
                points.append(value)
            for k, value in enumerate(dft8(points, -1)):
                for o in range(2):
                    tile(y_ref, o, k, row, lane_tile)[...] = value[o]
        for o in range(2):
            block = y_ref[o * 256:o * 256 + 256, cut].reshape(8, 4, 8, 128)
            tiles = [block[:, row].reshape(64, 128) for row in range(4)]
            for u, value in enumerate(swap_groups(tiles, lane)):
                out_ref[:, lane_tile * 4 + u, o * 8:o * 8 + 8, :] = value.reshape(8, 8, 128)
        here = slice(lane_tile * 4, lane_tile * 4 + 4)
        copy = pltpu.make_async_copy(
            out_ref.at[:, here], out_hbm.at[:, here], out_sems.at[lane_tile]
        )
        copy.start()
        outs.append(copy)
    for copy in outs:
        copy.wait()


def middle_kernel(
    counts_ref, x_hbm, table_hbm, twist_hbm, green_hbm, out_hbm,
    x_ref, table_ref, twist_ref, green_ref, out_ref, cells_ref, y_ref, sems, out_sems,
):
    copies = fetch(
        (x_hbm, table_hbm, twist_hbm, green_hbm), (x_ref, table_ref, twist_ref, green_ref), sems
    )
    copies[0].wait()

    def gather(device, start):
        for c in range(2):
            cells_ref[c, pl.ds(start, SLOTS)] = x_ref[device, c]
        return start + counts_ref[device]

    lax.fori_loop(0, DEVICES, gather, 0, unroll=8)
    w = [
        jnp.concatenate([cells_ref[c, 0:CELLS, h, :].T for h in range(2)], axis=0)
        for c in range(2)
    ]
    stacked = jnp.concatenate(
        [jnp.concatenate([w[0], w[1]], axis=1), jnp.concatenate([w[1], -w[0]], axis=1)], axis=0
    )
    copies[1].wait()
    y_ref[...] = dot3(stacked, table_ref)
    copies[2].wait()
    copies[3].wait()
    for lane_tile in range(4):
        cut = slice(lane_tile * 128, lane_tile * 128 + 128)
        for row in range(4):
            points = []
            for a in range(CELL):
                block = (a % 2) * 4 + a // 2
                value = tuple(tile(y_ref, o, block, row, lane_tile)[...] for o in range(2))
                if a:
                    value = twist(value, twist_ref[a:a + 1, cut], twist_ref[8 + a:9 + a, cut], -1)
                points.append(value)
            spectrum = []
            for q, value in enumerate(dft8(points, -1)):
                first = q * 512 + lane_tile * 128
                green = green_ref[row * 8:row * 8 + 8, first:first + 128]
                spectrum.append((value[0] * green, value[1] * green))
            for a, value in enumerate(dft8(spectrum, 1)):
                block = (a % 2) * 4 + a // 2
                if a:
                    value = twist(value, twist_ref[a:a + 1, cut], twist_ref[8 + a:9 + a, cut], 1)
                for o in range(2):
                    tile(y_ref, o, block, row, lane_tile)[...] = value[o]
    back = inverse_cells(y_ref, table_ref)
    for c in range(2):
        cells_ref[c, CELLS:] = jnp.zeros((8, 2, 128), F32)
        for h in range(2):
            first = (c * 2 + h) * 128
            cells_ref[c, 0:CELLS, h, :] = back[:, first:first + 128]

    slot = lax.broadcasted_iota(jnp.int32, (SLOTS, 2, 128), 0)

    def scatter(device, start):
        count = counts_ref[device]
        for c in range(2):
            held = cells_ref[c, pl.ds(start, SLOTS)]
            out_ref[device, c] = jnp.where(slot < count, held, 0.0)
        return start + count

    outs = []
    start = 0
    for part in range(4):
        here = slice(part * 32, part * 32 + 32)
        start = lax.fori_loop(part * 32, part * 32 + 32, scatter, start, unroll=8)
        copy = pltpu.make_async_copy(out_ref.at[here], out_hbm.at[here], out_sems.at[part])
        copy.start()
        outs.append(copy)
    for copy in outs:
        copy.wait()


def inverse_cells(y_ref, table_ref):
    re, im = y_ref[0:256, :], y_ref[256:512, :]
    by_cos = jnp.concatenate([re, im], axis=0)
    by_sin = jnp.concatenate([-im, re], axis=0)
    return dot3_nt(table_ref[0, 0:256, :], table_ref[1, 0:256, :], by_cos) + dot3_nt(
        table_ref[0, 256:512, :], table_ref[1, 256:512, :], by_sin
    )


def backward_kernel(
    x_hbm, whole_hbm, part_hbm, order_hbm, table_hbm, twist_hbm, out_hbm,
    x_ref, part_ref, order_ref, table_ref, twist_ref, out_ref, y_ref, sems, out_sems,
):
    copies = fetch(
        (x_hbm, twist_hbm, table_hbm, order_hbm, part_hbm),
        (x_ref, twist_ref, table_ref, order_ref, part_ref),
        sems,
    )
    lane = lax.broadcasted_iota(jnp.int32, (64, 128), 1)
    copies[0].wait()
    copies[1].wait()
    for lane_tile in range(4):
        cut = slice(lane_tile * 128, lane_tile * 128 + 128)
        for o in range(2):
            tiles = [
                x_ref[:, lane_tile * 4 + u, o * 8:o * 8 + 8, :].reshape(64, 128) for u in range(4)
            ]
            for row, value in enumerate(swap_groups(tiles, lane)):
                for k in range(CELL):
                    tile(y_ref, o, k, row, lane_tile)[...] = value[k * 8:k * 8 + 8, :]
        for row in range(4):
            points = [
                tuple(tile(y_ref, o, k, row, lane_tile)[...] for o in range(2))
                for k in range(CELL)
            ]
            for b, value in enumerate(dft8(points, 1)):
                if b:
                    value = twist(value, twist_ref[b:b + 1, cut], twist_ref[8 + b:9 + b, cut], 1)
                for o in range(2):
                    tile(y_ref, o, b, row, lane_tile)[...] = value[o]
    copies[2].wait()
    back = inverse_cells(y_ref, table_ref)
    copies[3].wait()
    copies[4].wait()
    halves = [split(back[:, c * 256:c * 256 + 256]) for c in range(2)]
    outs = []
    for slot in range(SLOTS):
        order = order_ref[:, slot * 128:slot * 128 + 128]
        for c in range(2):
            plane = dot(halves[c][0], order) + dot(halves[c][1], order)
            out_ref[slot, :, c, :] = part_ref[slot, c] + plane
        copy = pltpu.make_async_copy(
            out_ref.at[slot], out_hbm.at[slot, :, :, 0:128], out_sems.at[slot]
        )
        copy.start()
        outs.append(copy)
    for copy in outs:
        copy.wait()


def edge_kernel(counts_ref, x_hbm, first_hbm, last_hbm, first_ref, last_ref, sems, out_sems):
    count = counts_ref[lax.axis_index("row")]
    ins = fetch((x_hbm.at[0:1], x_hbm.at[pl.ds(count - 1, 1)]), (first_ref, last_ref), sems)
    outs = []
    for n, (held, target) in enumerate(((first_ref, first_hbm), (last_ref, last_hbm))):
        ins[n].wait()
        copy = pltpu.make_async_copy(held, target, out_sems.at[n])
        copy.start()
        outs.append(copy)
    for copy in outs:
        copy.wait()


def structural_kernel(
    counts_ref, x_hbm, above_hbm, below_hbm, stiff_hbm, couple_ref, soft_ref, mask_ref,
    out_hbm, part_hbm, x_ref, above_ref, below_ref, stiff_ref, plane_ref, part_ref, sems, out_sems,
):
    count = counts_ref[lax.axis_index("row")]
    copies = fetch(
        [stiff_hbm, above_hbm, below_hbm] + [x_hbm.at[slot] for slot in range(SLOTS)],
        [stiff_ref, above_ref, below_ref] + [x_ref.at[slot] for slot in range(SLOTS)],
        sems,
    )
    for slot in range(SLOTS):
        copies[3 + slot].wait()
        for c in range(2):
            plane_ref[slot + 1, c] = x_ref[slot, :, c, :]
    for copy in copies[:3]:
        copy.wait()
    for c in range(2):
        plane_ref[0, c] = above_ref[0, :, c, :]
        plane_ref[count + 1, c] = below_ref[0, :, c, :]
    outs = []
    cell = lax.broadcasted_iota(jnp.int32, (CELLS, 1), 0)
    for slot in range(SLOTS):
        biased = mask_ref[:, slot:slot + 1]
        for c in range(2):
            own = plane_ref[slot + 1, c]
            elastic = dot(own.astype(BF16), stiff_ref[...])
            left = jnp.where(cell == 0, 0.0, pltpu.roll(own, 1, 0))
            right = jnp.where(cell == CELLS - 1, 0.0, pltpu.roll(own, CELLS - 1, 0))
            beside = plane_ref[slot, c] + plane_ref[slot + 2, c] + left + right
            value = elastic - couple_ref[...] * beside - (biased * soft_ref[...]) * own
            value = jnp.where(slot < count, value, 0.0)
            part_ref[slot, c] = value[:, 0:128]
            x_ref[slot, :, c, :] = value
        copy = pltpu.make_async_copy(x_ref.at[slot], out_hbm.at[slot], out_sems.at[slot])
        copy.start()
        outs.append(copy)
    copy = pltpu.make_async_copy(part_ref, part_hbm, out_sems.at[SLOTS])
    copy.start()
    outs.append(copy)
    for copy in outs:
        copy.wait()


HBM = pl.BlockSpec(memory_space=pltpu.HBM)
SCALARS = pl.BlockSpec(memory_space=pltpu.SMEM)
VECTORS = pl.BlockSpec(memory_space=pltpu.VMEM)
CHUNK = (DEVICES, 16, 128)
ORDER = pltpu.VMEM((256, 512), BF16)
TABLE = pltpu.VMEM((2, 512, 512), BF16)
TURNS = pltpu.VMEM((16, 512), F32)
SPECTRAL = pltpu.VMEM((512, 512), F32)
BLOCK = (SLOTS, CELLS, 2, 384)
EDGE = (1, CELLS, 2, 384)
PARAMS = pltpu.CompilerParams(vmem_limit_bytes=VMEM_LIMIT)


def dma(count):
    return pltpu.SemaphoreType.DMA((count,))


def cost(flops, size):
    return pl.CostEstimate(flops=flops, bytes_accessed=size, transcendentals=0)


def forward(displacement, table, turns):
    shape = (8, 16, 16, 128)
    sent = pl.pallas_call(
        forward_kernel,
        in_specs=[HBM] * 4,
        out_specs=HBM,
        out_shape=jax.ShapeDtypeStruct(shape, F32),
        scratch_shapes=[
            pltpu.VMEM(BLOCK, F32), ORDER, TABLE, TURNS, pltpu.VMEM(shape, F32), SPECTRAL,
            dma(7), dma(4),
        ],
        compiler_params=PARAMS,
        cost_estimate=cost(10**9, 4 << 20),
    )(displacement, jnp.asarray(dof_order_table(1.0)), table, turns)
    return sent.reshape(CHUNK)


def middle(received, row_counts, table, turns, green_spectrum):
    shape = (DEVICES, 2, SLOTS, 2, 128)
    sent = pl.pallas_call(
        middle_kernel,
        in_specs=[SCALARS] + [HBM] * 4,
        out_specs=HBM,
        out_shape=jax.ShapeDtypeStruct(shape, F32),
        scratch_shapes=[
            pltpu.VMEM(shape, F32), TABLE, TURNS, pltpu.VMEM((32, PAD), F32),
            pltpu.VMEM(shape, F32), pltpu.VMEM((2, CELLS + 8, 2, 128), F32), SPECTRAL,
            dma(4), dma(4),
        ],
        compiler_params=PARAMS,
        cost_estimate=cost(3 * 10**9, 5 << 20),
    )(row_counts, received.reshape(shape), table, turns, green_spectrum)
    return sent.reshape(CHUNK)


def backward(received, structural, part, table, turns):
    return pl.pallas_call(
        backward_kernel,
        in_specs=[HBM] * 6,
        out_specs=HBM,
        out_shape=jax.ShapeDtypeStruct(BLOCK, F32),
        scratch_shapes=[
            pltpu.VMEM((8, 16, 16, 128), F32), pltpu.VMEM((SLOTS, 2, CELLS, 128), F32), ORDER, TABLE,
            TURNS,
            pltpu.VMEM((SLOTS, CELLS, 2, 128), F32), SPECTRAL, dma(5), dma(4),
        ],
        input_output_aliases={1: 0},
        compiler_params=PARAMS,
        cost_estimate=cost(10**9, 4 << 20),
    )(
        received.reshape(8, 16, 16, 128), structural, part,
        jnp.asarray(dof_order_table(1.0 / (PAD * PAD))), table, turns,
    )


def edge_rows(displacement, row_counts):
    return pl.pallas_call(
        edge_kernel,
        in_specs=[SCALARS, HBM],
        out_specs=[HBM] * 2,
        out_shape=[jax.ShapeDtypeStruct(EDGE, F32)] * 2,
        scratch_shapes=[pltpu.VMEM(EDGE, F32), pltpu.VMEM(EDGE, F32), dma(2), dma(2)],
        compiler_params=PARAMS,
        cost_estimate=cost(0, 3 << 20),
    )(row_counts, displacement)


def structure(
    displacement, above, below, stiffness, coupling, softening, biased, row_counts
):
    return pl.pallas_call(
        structural_kernel,
        in_specs=[SCALARS] + [HBM] * 4 + [VECTORS] * 3,
        out_specs=[HBM] * 2,
        out_shape=[
            jax.ShapeDtypeStruct(BLOCK, F32),
            jax.ShapeDtypeStruct((SLOTS, 2, CELLS, 128), F32),
        ],
        scratch_shapes=[
            pltpu.VMEM(BLOCK, F32), pltpu.VMEM(EDGE, F32), pltpu.VMEM(EDGE, F32),
            pltpu.VMEM((384, 384), BF16), pltpu.VMEM((SLOTS + 2, 2, CELLS, 384), F32),
            pltpu.VMEM((SLOTS, 2, CELLS, 128), F32), dma(7), dma(5),
        ],
        compiler_params=PARAMS,
        cost_estimate=cost(10**9, 8 << 20),
    )(row_counts, displacement, above, below, stiffness, coupling, softening, biased)


def per_device(
    displacement, stiffness, coupling, softening, electrode_mask, row_counts, green_spectrum
):
    table = jnp.asarray(dft_table())
    turns = jnp.asarray(twiddle_table())
    devices = lax.axis_size("row")
    up = [(i, i + 1) for i in range(devices - 1)]
    down = [(j, i) for i, j in up]
    first, last = edge_rows(displacement, row_counts)
    above = lax.ppermute(last, "row", up)
    below = lax.ppermute(first, "row", down)
    sent = forward(displacement, table, turns)
    sent, above, below = lax.optimization_barrier((sent, above, below))
    received = lax.all_to_all(sent, "row", split_axis=0, concat_axis=0, tiled=True)
    structural, part = structure(
        displacement, above, below, stiffness, coupling[None, :], softening[None, :],
        electrode_mask.astype(F32).T, row_counts,
    )
    received, structural, part = lax.optimization_barrier((received, structural, part))
    sent = middle(received, row_counts, table, turns, green_spectrum)
    received = lax.all_to_all(sent, "row", split_axis=0, concat_axis=0, tiled=True)
    return backward(received, structural, part, table, turns)


def solution(mesh):
    placed = (P("row", None, None, None), P(), P(), P(), P("row", None), P(), P("row", None))
    return jax.shard_map(
        per_device,
        mesh=mesh,
        in_specs=placed,
        out_specs=P("row", None, None, None),
        check_vma=False,
    )
```

time: 104 us -> 90.5 us (0.87)
  the two profiles are of different devices: /device:TPU:24 before, /device:TPU:1 now
where the time goes in v2:
time: 90.5 us; the launch traced here: 90.1 us
  Pallas kernels  28.4 us (31%)
  blocking collectives  24.9 us (28%)
  starting transfers between devices  19 us (21%)
  waiting for transfers between devices  14.9 us (16%)
  local copies, waits for them, and re-layouts  2.98 us (3%)
    all_to_all x1, blocking collectives, per_device(): lax.all_to_all(sent, 'row', split_axis=0, concat_axis=0, tiled=True)  24.9 us
    all_to_all x1, starting transfers between devices, per_device(): lax.all_to_all(sent, 'row', split_axis=0, concat_axis=0, tiled=True)  12 us
    all_to_all x1, waiting for transfers between devices, per_device(): lax.all_to_all(sent, 'row', split_axis=0, concat_axis=0, tiled=True)  9.29 us
    pallas_call x1, Pallas kernels, structure(): pl.pallas_call(structural_kernel, in_specs=[SCALARS] + [HBM] * 4 + [VECTO...  7.87 us
    pallas_call x1, Pallas kernels, middle(): pl.pallas_call(middle_kernel, in_specs=[SCALARS] + [HBM] * 4, out_specs=H...  6.52 us
    pallas_call x1, Pallas kernels, forward(): pl.pallas_call(forward_kernel, in_specs=[HBM] * 4, out_specs=HBM, out_sha...  6 us
    pallas_call x1, Pallas kernels, backward(): pl.pallas_call(backward_kernel, in_specs=[HBM] * 6, out_specs=HBM, out_sh...  4.97 us
    ppermute x1, starting transfers between devices, per_device(): above = lax.ppermute(last, 'row', up)  4.94 us
  transfers between devices with their start and end apart: 3, of which 3 were waited for; matrix products, arithmetic and copies ran while one was open for 2% of the time, Pallas kernels for 15%

profile of v2, /device:TPU:1, one launch (start us, length us, event | category | flops | bytes accessed | tf_op | source)
XLA Modules:
  0.0 90.1 jit_solution(1828830431069491946)
XLA Ops:
  0.0 3.0 %shard_map.110 = (f32[1,256,2,384]{3,2,1,0:T(2,128)}, f32[1,256,2,384]{3,2,1,0:T(2,128)}) custom-call(s32[128]{0:T(128)} %counts_ref.5, f32[4,256,2,384]{3,2,1,0:T(2,128)} %x_hbm.5), custom_call_target="tpu_custom_call" | custom-call | bytes 3145728 | tf_op jit(solution)/shard_map/pallas_call | solution.py:467
  3.0 4.9 %collective-permute-start = (f32[1,256,2,384]{3,2,1,0:T(2,128)}, f32[1,256,2,384]{3,2,1,0:T(2,128)S(1)}, u32[]{:S(2)}, u32[]{:S(2)}) collective-permute-start(f32[1,256,2,384]{3,2,1,0:T(2,128)} %get-tuple-element.15), channel_id=1, source_target_pairs={{0,1},{1,2},{2,3},{3,4},{4,5},{5,6},{6,7},{7,8},{8,9},{9,10},{10,1... | collective-permute-start | bytes 2359304 | tf_op jit(solution)/shard_map/ppermute | solution.py:508
  8.0 0.0 copy-start.4
  8.0 0.0 copy-start.5
  8.0 0.0 copy-start.3
  8.0 2.1 %collective-permute-start.1 = (f32[1,256,2,384]{3,2,1,0:T(2,128)}, f32[1,256,2,384]{3,2,1,0:T(2,128)S(1)}, u32[]{:S(2)}, u32[]{:S(2)}) collective-permute-start(f32[1,256,2,384]{3,2,1,0:T(2,128)} %get-tuple-element.16), channel_id=1, source_target_pairs={{1,0},{2,1},{3,2},{4,3},{5,4},{6,5},{7,6},{8,7},{9,8},{10,9},{11,1... | collective-permute-start | bytes 2359304 | tf_op jit(solution)/shard_map/ppermute | solution.py:509
  10.1 6.0 %shard_map.109 = f32[8,16,16,128]{3,2,1,0:T(8,128)} custom-call(f32[4,256,2,384]{3,2,1,0:T(2,128)} %x_hbm.5, bf16[256,512]{1,0:T(8,128)(2,1)} %constant.10.clone.order_hbm, bf16[2,512,512]{2,1,0:T(8,128)(2,1)} %constant.8.clone.table_hbm, f32[16,512]{1,0:T(8,128)} %constant.9.clone.twist_hbm), custom_call_target="tpu_custom_call" | custom-call | flops 1000000000 | bytes 4194304 | tf_op jit(solution)/shard_map/pallas_call | solution.py:413
  16.1 1.1 %collective-permute-done.above_hbm = f32[1,256,2,384]{3,2,1,0:T(2,128)S(1)} collective-permute-done((f32[1,256,2,384]{3,2,1,0:T(2,128)}, f32[1,256,2,384]{3,2,1,0:T(2,128)S(1)}, u32[]{:S(2)}, u32[]{:S(2)}) %collective-permute-start) | collective-permute-done | bytes 786464 | tf_op jit(solution)/shard_map/ppermute | solution.py:508
  17.2 0.0 copy-start.1
  17.2 4.5 %collective-permute-done.1.below_hbm = f32[1,256,2,384]{3,2,1,0:T(2,128)S(1)} collective-permute-done((f32[1,256,2,384]{3,2,1,0:T(2,128)}, f32[1,256,2,384]{3,2,1,0:T(2,128)S(1)}, u32[]{:S(2)}, u32[]{:S(2)}) %collective-permute-start.1) | collective-permute-done | bytes 786464 | tf_op jit(solution)/shard_map/ppermute | solution.py:509
  21.7 0.0 copy-start.2
  21.7 12.0 %all-to-all-start = ((f32[128,16,128]{2,1,0:T(8,128)}), f32[128,16,128]{2,1,0:T(8,128)S(1)}, u32[]{:S(2)}, u32[]{:S(2)}) async-start(f32[128,16,128]{2,1,0:T(8,128)} %bitcast.6), calls=%async_computation | async-start | bytes 2097152 | tf_op jit(solution)/shard_map/all_to_all | solution.py:512
  33.6 0.0 copy-done.4
  33.6 0.6 broadcast_in_dim.6.couple_ref
  34.2 0.0 copy-done.5
  34.2 0.6 broadcast_in_dim.7.soft_ref
  34.8 0.0 copy-done.3
  34.8 0.8 copy.13
  35.6 0.0 copy-done.1
  35.6 0.0 copy-done.2
  35.6 7.9 %shard_map.111 = (f32[4,256,2,384]{3,2,1,0:T(2,128)}, f32[4,2,256,128]{3,2,1,0:T(8,128)}) custom-call(s32[128]{0:T(128)} %counts_ref.5, f32[4,256,2,384]{3,2,1,0:T(2,128)} %x_hbm.5, f32[1,256,2,384]{3,2,1,0:T(2,128)} %copy-done.1, f32[1,256,2,384]{3,2,1,0:T(2,128)} %copy-done.2, bf16[384,384]{1,0:T(8,128)(2,1)} %stiff_hbm.1, ...), custom_call_target="tpu_custom_call" | custom-call | flops 1000000000 | bytes 8388608 | tf_op jit(solution)/shard_map/pallas_call | solution.py:481
  43.5 9.3 %all-to-all-done = f32[128,16,128]{2,1,0:T(8,128)S(1)} async-done(((f32[128,16,128]{2,1,0:T(8,128)}), f32[128,16,128]{2,1,0:T(8,128)S(1)}, u32[]{:S(2)}, u32[]{:S(2)}) %all-to-all-start) | async-done | bytes 1048608 | tf_op jit(solution)/shard_map/all_to_all | solution.py:512
  52.8 0.0 copy-start
  52.8 1.0 %copy-done = f32[128,16,128]{2,1,0:T(8,128)} copy-done((f32[128,16,128]{2,1,0:T(8,128)}, f32[128,16,128]{2,1,0:T(8,128)S(1)}, u32[]{:S(2)}) %copy-start) | copy-done | bytes 1048600
  53.8 6.5 %shard_map.112 = f32[128,2,4,2,128]{4,3,2,1,0:T(2,128)} custom-call(s32[128]{0:T(128)} %counts_ref.5, f32[128,2,4,2,128]{4,3,2,1,0:T(2,128)} %bitcast.7, bf16[2,512,512]{2,1,0:T(8,128)(2,1)} %constant.8.clone.table_hbm, f32[16,512]{1,0:T(8,128)} %constant.9.clone.twist_hbm, f32[32,4096]{1,0:T(8,128)} %green_hbm.1), custom_call_target="tpu_custom_call" | custom-call | flops 3000000000 | bytes 5242880 | tf_op jit(solution)/shard_map/pallas_call | solution.py:430
  60.3 24.9 %all_to_all.10 = f32[128,16,128]{2,1,0:T(8,128)} all-to-all(f32[128,16,128]{2,1,0:T(8,128)} %bitcast.8), channel_id=1, replica_groups=mesh['row'=128] {'row'}, dimensions={0} | all-to-all | bytes 2097152 | tf_op jit(solution)/shard_map/all_to_all | solution.py:519
  85.2 5.0 %shard_map.113 = f32[4,256,2,384]{3,2,1,0:T(2,128)} custom-call(f32[8,16,16,128]{3,2,1,0:T(8,128)} %bitcast.5, f32[4,256,2,384]{3,2,1,0:T(2,128)} %get-tuple-element.23.whole_hbm, f32[4,2,256,128]{3,2,1,0:T(8,128)} %get-tuple-element.24.part_hbm, bf16[256,512]{1,0:T(8,128)(2,1)} %constant.11.clone.order_hbm, ...), custom_call_target="tpu_custom_call", output_to_operand_aliasing={{}: (1, {})} | custom-call | flops 1000000000 | bytes 4194304 | tf_op jit(solution)/shard_map/pallas_call | solution.py:447
  (1 shorter events, 0.0 us)
Async XLA Ops:
  3.0 14.2 %collective-permute-start = (f32[1,256,2,384]{3,2,1,0:T(2,128)}, f32[1,256,2,384]{3,2,1,0:T(2,128)S(1)}, u32[]{:S(2)}, u32[]{:S(2)}) collective-permute-start(f32[1,256,2,384]{3,2,1,0:T(2,128)} %get-tuple-element.15), channel_id=1, source_target_pairs={{0,1},{1,2},{2,3},{3,4},{4,5},{5,6},{6,7},{7,8},{8,9},{9,10},{10,1... | collective-permute-start | bytes 2359304 | tf_op jit(solution)/shard_map/ppermute | solution.py:508
  8.0 25.7 %copy-start.4 = (f32[384]{0:T(512)S(1)}, f32[384]{0:T(512)}, u32[]{:S(2)}) copy-start(f32[384]{0:T(512)} %param.13) | copy-start | bytes 4612
  8.0 26.3 %copy-start.5 = (f32[384]{0:T(512)S(1)}, f32[384]{0:T(512)}, u32[]{:S(2)}) copy-start(f32[384]{0:T(512)} %param.14) | copy-start | bytes 4612
  8.0 26.8 %copy-start.3 = (s32[4,256]{1,0:T(4,128)S(1)}, s32[4,256]{1,0:T(4,128)}, u32[]{:S(2)}) copy-start(s32[4,256]{1,0:T(4,128)} %param.15) | copy-start | bytes 12292
  8.0 13.7 %collective-permute-start.1 = (f32[1,256,2,384]{3,2,1,0:T(2,128)}, f32[1,256,2,384]{3,2,1,0:T(2,128)S(1)}, u32[]{:S(2)}, u32[]{:S(2)}) collective-permute-start(f32[1,256,2,384]{3,2,1,0:T(2,128)} %get-tuple-element.16), channel_id=1, source_target_pairs={{1,0},{2,1},{3,2},{4,3},{5,4},{6,5},{7,6},{8,7},{9,8},{10,9},{11,1... | collective-permute-start | bytes 2359304 | tf_op jit(solution)/shard_map/ppermute | solution.py:509
  17.2 18.4 %copy-start.1 = (f32[1,256,2,384]{3,2,1,0:T(2,128)}, f32[1,256,2,384]{3,2,1,0:T(2,128)S(1)}, u32[]{:S(2)}) copy-start(f32[1,256,2,384]{3,2,1,0:T(2,128)S(1)} %collective-permute-done.above_hbm) | copy-start | bytes 2359300
  21.7 14.0 %copy-start.2 = (f32[1,256,2,384]{3,2,1,0:T(2,128)}, f32[1,256,2,384]{3,2,1,0:T(2,128)S(1)}, u32[]{:S(2)}) copy-start(f32[1,256,2,384]{3,2,1,0:T(2,128)S(1)} %collective-permute-done.1.below_hbm) | copy-start | bytes 2359300
  21.7 31.1 %all-to-all-start = ((f32[128,16,128]{2,1,0:T(8,128)}), f32[128,16,128]{2,1,0:T(8,128)S(1)}, u32[]{:S(2)}, u32[]{:S(2)}) async-start(f32[128,16,128]{2,1,0:T(8,128)} %bitcast.6), calls=%async_computation | async-start | bytes 2097152 | tf_op jit(solution)/shard_map/all_to_all | solution.py:512
  52.8 1.0 %copy-start = (f32[128,16,128]{2,1,0:T(8,128)}, f32[128,16,128]{2,1,0:T(8,128)S(1)}, u32[]{:S(2)}) copy-start(f32[128,16,128]{2,1,0:T(8,128)S(1)} %all-to-all-done) | copy-start | bytes 3145732

commit v3 on v2

--- a/solution.py
+++ b/solution.py
@@ -145,30 +145,39 @@
 
 
 def forward_kernel(
-    x_hbm, order_hbm, table_hbm, twist_hbm, out_hbm,
-    x_ref, order_ref, table_ref, twist_ref, out_ref, y_ref, sems, out_sems,
+    counts_ref, x_hbm, order_hbm, table_hbm, twist_hbm, out_hbm, first_hbm, last_hbm,
+    x_ref, order_ref, table_ref, twist_ref, out_ref, first_ref, last_ref, y_ref, sems, out_sems,
 ):
+    count = counts_ref[lax.axis_index("row")]
     copies = fetch(
-        [x_hbm.at[slot] for slot in range(SLOTS)] + [order_hbm, table_hbm, twist_hbm],
-        [x_ref.at[slot] for slot in range(SLOTS)] + [order_ref, table_ref, twist_ref],
+        (
+            order_hbm, x_hbm.at[:, :, :, 0:128], table_hbm, twist_hbm,
+            x_hbm.at[0:1], x_hbm.at[pl.ds(count - 1, 1)],
+        ),
+        (order_ref, x_ref, table_ref, twist_ref, first_ref, last_ref),
         sems,
     )
-    for copy in copies[:5]:
-        copy.wait()
+    copies[0].wait()
+    copies[1].wait()
     planes = []
     for c in range(2):
-        plane = jnp.concatenate([x_ref[slot, :, c, 0:128] for slot in range(SLOTS)], axis=1)
+        plane = jnp.concatenate([x_ref[slot, :, c, :] for slot in range(SLOTS)], axis=1)
         high, low = split(plane)
         planes.append(dot_nt(order_ref[...], high) + dot_nt(order_ref[...], low))
     w0, w1 = planes
     stacked = jnp.concatenate(
         [jnp.concatenate([w0, w1], axis=1), jnp.concatenate([w1, -w0], axis=1)], axis=0
     )
-    copies[5].wait()
+    copies[2].wait()
     y_ref[...] = dot3(stacked, table_ref)
-    copies[6].wait()
+    copies[3].wait()
     lane = lax.broadcasted_iota(jnp.int32, (64, 128), 1)
     outs = []
+    for n, (held, target) in enumerate(((first_ref, first_hbm), (last_ref, last_hbm))):
+        copies[4 + n].wait()
+        copy = pltpu.make_async_copy(held, target, out_sems.at[4 + n])
+        copy.start()
+        outs.append(copy)
     for lane_tile in range(4):
         cut = slice(lane_tile * 128, lane_tile * 128 + 128)
         for row in range(4):
@@ -281,12 +290,24 @@
 
 
 def backward_kernel(
-    x_hbm, whole_hbm, part_hbm, order_hbm, table_hbm, twist_hbm, out_hbm,
-    x_ref, part_ref, order_ref, table_ref, twist_ref, out_ref, y_ref, sems, out_sems,
+    counts_ref, x_hbm, whole_hbm, part_hbm, above_hbm, below_hbm, couple_hbm, order_hbm,
+    table_hbm, twist_hbm, out_hbm,
+    x_ref, part_ref, above_ref, below_ref, couple_ref, first_ref, last_ref, order_ref,
+    table_ref, twist_ref, out_ref, y_ref, sems, out_sems,
 ):
+    count = counts_ref[lax.axis_index("row")]
+    rest = slice(128, 384)
+    first_row = whole_hbm.at[0, :, :, rest]
+    last_row = whole_hbm.at[count - 1, :, :, rest]
     copies = fetch(
-        (x_hbm, twist_hbm, table_hbm, order_hbm, part_hbm),
-        (x_ref, twist_ref, table_ref, order_ref, part_ref),
+        (
+            x_hbm, twist_hbm, table_hbm, order_hbm, part_hbm,
+            above_hbm, below_hbm, couple_hbm, first_row, last_row,
+        ),
+        (
+            x_ref, twist_ref, table_ref, order_ref, part_ref,
+            above_ref, below_ref, couple_ref, first_ref, last_ref,
+        ),
         sems,
     )
     lane = lax.broadcasted_iota(jnp.int32, (64, 128), 1)
@@ -314,55 +335,62 @@
     copies[2].wait()
     back = inverse_cells(y_ref, table_ref)
     copies[3].wait()
-    copies[4].wait()
+    for copy in copies[4:]:
+        copy.wait()
+    alone = count == 1
+    couple = couple_ref[:, rest]
+    last_ref[...] = last_ref[...] - couple * (
+        below_ref[0, :, :, rest] + jnp.where(alone, above_ref[0, :, :, rest], 0.0)
+    )
+    last_copy = pltpu.make_async_copy(
+        last_ref, out_hbm.at[count - 1, :, :, rest], out_sems.at[SLOTS]
+    )
+    last_copy.start()
+    first_ref[...] = first_ref[...] - couple * (
+        above_ref[0, :, :, rest] + jnp.where(alone, below_ref[0, :, :, rest], 0.0)
+    )
+    near = couple_ref[0:1, 0:128]
     halves = [split(back[:, c * 256:c * 256 + 256]) for c in range(2)]
     outs = []
     for slot in range(SLOTS):
         order = order_ref[:, slot * 128:slot * 128 + 128]
         for c in range(2):
             plane = dot(halves[c][0], order) + dot(halves[c][1], order)
-            out_ref[slot, :, c, :] = part_ref[slot, c] + plane
+            beside = jnp.where(slot == count - 1, below_ref[0, :, c, 0:128], 0.0)
+            if slot == 0:
+                beside = beside + above_ref[0, :, c, 0:128]
+            out_ref[slot, :, c, :] = part_ref[slot, c] + plane - near * beside
         copy = pltpu.make_async_copy(
             out_ref.at[slot], out_hbm.at[slot, :, :, 0:128], out_sems.at[slot]
         )
         copy.start()
         outs.append(copy)
+    last_copy.wait()
+    copy = pltpu.make_async_copy(first_ref, out_hbm.at[0, :, :, rest], out_sems.at[SLOTS + 1])
+    copy.start()
+    outs.append(copy)
     for copy in outs:
         copy.wait()
 
 
-def edge_kernel(counts_ref, x_hbm, first_hbm, last_hbm, first_ref, last_ref, sems, out_sems):
-    count = counts_ref[lax.axis_index("row")]
-    ins = fetch((x_hbm.at[0:1], x_hbm.at[pl.ds(count - 1, 1)]), (first_ref, last_ref), sems)
-    outs = []
-    for n, (held, target) in enumerate(((first_ref, first_hbm), (last_ref, last_hbm))):
-        ins[n].wait()
-        copy = pltpu.make_async_copy(held, target, out_sems.at[n])
-        copy.start()
-        outs.append(copy)
-    for copy in outs:
-        copy.wait()
-
-
 def structural_kernel(
-    counts_ref, x_hbm, above_hbm, below_hbm, stiff_hbm, couple_ref, soft_ref, mask_ref,
-    out_hbm, part_hbm, x_ref, above_ref, below_ref, stiff_ref, plane_ref, part_ref, sems, out_sems,
+    counts_ref, x_hbm, stiff_hbm, couple_ref, soft_ref, mask_ref, out_hbm, part_hbm,
+    x_ref, stiff_ref, plane_ref, part_ref, sems, out_sems,
 ):
     count = counts_ref[lax.axis_index("row")]
     copies = fetch(
-        [stiff_hbm, above_hbm, below_hbm] + [x_hbm.at[slot] for slot in range(SLOTS)],
-        [stiff_ref, above_ref, below_ref] + [x_ref.at[slot] for slot in range(SLOTS)],
+        [stiff_hbm] + [x_hbm.at[slot] for slot in range(SLOTS)],
+        [stiff_ref] + [x_ref.at[slot] for slot in range(SLOTS)],
         sems,
     )
     for slot in range(SLOTS):
-        copies[3 + slot].wait()
+        copies[1 + slot].wait()
         for c in range(2):
             plane_ref[slot + 1, c] = x_ref[slot, :, c, :]
-    for copy in copies[:3]:
-        copy.wait()
+    copies[0].wait()
     for c in range(2):
-        plane_ref[0, c] = above_ref[0, :, c, :]
-        plane_ref[count + 1, c] = below_ref[0, :, c, :]
+        plane_ref[0, c] = jnp.zeros((CELLS, 384), F32)
+        plane_ref[count + 1, c] = jnp.zeros((CELLS, 384), F32)
     outs = []
     cell = lax.broadcasted_iota(jnp.int32, (CELLS, 1), 0)
     for slot in range(SLOTS):
@@ -408,21 +436,25 @@
     return pl.CostEstimate(flops=flops, bytes_accessed=size, transcendentals=0)
 
 
-def forward(displacement, table, turns):
+def forward(displacement, row_counts, table, turns):
     shape = (8, 16, 16, 128)
-    sent = pl.pallas_call(
+    sent, first, last = pl.pallas_call(
         forward_kernel,
-        in_specs=[HBM] * 4,
-        out_specs=HBM,
-        out_shape=jax.ShapeDtypeStruct(shape, F32),
+        in_specs=[SCALARS] + [HBM] * 4,
+        out_specs=[HBM] * 3,
+        out_shape=[
+            jax.ShapeDtypeStruct(shape, F32),
+            jax.ShapeDtypeStruct(EDGE, F32),
+            jax.ShapeDtypeStruct(EDGE, F32),
+        ],
         scratch_shapes=[
-            pltpu.VMEM(BLOCK, F32), ORDER, TABLE, TURNS, pltpu.VMEM(shape, F32), SPECTRAL,
-            dma(7), dma(4),
+            pltpu.VMEM((SLOTS, CELLS, 2, 128), F32), ORDER, TABLE, TURNS, pltpu.VMEM(shape, F32),
+            pltpu.VMEM(EDGE, F32), pltpu.VMEM(EDGE, F32), SPECTRAL, dma(6), dma(6),
         ],
         compiler_params=PARAMS,
-        cost_estimate=cost(10**9, 4 << 20),
-    )(displacement, jnp.asarray(dof_order_table(1.0)), table, turns)
-    return sent.reshape(CHUNK)
+        cost_estimate=cost(10**9, 7 << 20),
+    )(row_counts, displacement, jnp.asarray(dof_order_table(1.0)), table, turns)
+    return sent.reshape(CHUNK), first, last
 
 
 def middle(received, row_counts, table, turns, green_spectrum):
@@ -443,57 +475,45 @@
     return sent.reshape(CHUNK)
 
 
-def backward(received, structural, part, table, turns):
+def backward(received, structural, part, above, below, coupling, row_counts, table, turns):
+    edge = pltpu.VMEM((CELLS, 2, 256), F32)
     return pl.pallas_call(
         backward_kernel,
-        in_specs=[HBM] * 6,
+        in_specs=[SCALARS] + [HBM] * 9,
         out_specs=HBM,
         out_shape=jax.ShapeDtypeStruct(BLOCK, F32),
         scratch_shapes=[
-            pltpu.VMEM((8, 16, 16, 128), F32), pltpu.VMEM((SLOTS, 2, CELLS, 128), F32), ORDER, TABLE,
-            TURNS,
-            pltpu.VMEM((SLOTS, CELLS, 2, 128), F32), SPECTRAL, dma(5), dma(4),
+            pltpu.VMEM((8, 16, 16, 128), F32), pltpu.VMEM((SLOTS, 2, CELLS, 128), F32),
+            pltpu.VMEM(EDGE, F32), pltpu.VMEM(EDGE, F32), pltpu.VMEM((2, 384), F32), edge, edge,
+            ORDER, TABLE, TURNS, pltpu.VMEM((SLOTS, CELLS, 2, 128), F32), SPECTRAL,
+            dma(10), dma(SLOTS + 2),
         ],
-        input_output_aliases={1: 0},
+        input_output_aliases={2: 0},
         compiler_params=PARAMS,
-        cost_estimate=cost(10**9, 4 << 20),
+        cost_estimate=cost(10**9, 8 << 20),
     )(
-        received.reshape(8, 16, 16, 128), structural, part,
+        row_counts, received.reshape(8, 16, 16, 128), structural, part, above, below, coupling,
         jnp.asarray(dof_order_table(1.0 / (PAD * PAD))), table, turns,
     )
 
 
-def edge_rows(displacement, row_counts):
-    return pl.pallas_call(
-        edge_kernel,
-        in_specs=[SCALARS, HBM],
-        out_specs=[HBM] * 2,
-        out_shape=[jax.ShapeDtypeStruct(EDGE, F32)] * 2,
-        scratch_shapes=[pltpu.VMEM(EDGE, F32), pltpu.VMEM(EDGE, F32), dma(2), dma(2)],
-        compiler_params=PARAMS,
-        cost_estimate=cost(0, 3 << 20),
-    )(row_counts, displacement)
-
-
-def structure(
-    displacement, above, below, stiffness, coupling, softening, biased, row_counts
-):
+def structure(displacement, stiffness, coupling, softening, biased, row_counts):
     return pl.pallas_call(
         structural_kernel,
-        in_specs=[SCALARS] + [HBM] * 4 + [VECTORS] * 3,
+        in_specs=[SCALARS] + [HBM] * 2 + [VECTORS] * 3,
         out_specs=[HBM] * 2,
         out_shape=[
             jax.ShapeDtypeStruct(BLOCK, F32),
             jax.ShapeDtypeStruct((SLOTS, 2, CELLS, 128), F32),
         ],
         scratch_shapes=[
-            pltpu.VMEM(BLOCK, F32), pltpu.VMEM(EDGE, F32), pltpu.VMEM(EDGE, F32),
-            pltpu.VMEM((384, 384), BF16), pltpu.VMEM((SLOTS + 2, 2, CELLS, 384), F32),
-            pltpu.VMEM((SLOTS, 2, CELLS, 128), F32), dma(7), dma(5),
+            pltpu.VMEM(BLOCK, F32), pltpu.VMEM((384, 384), BF16),
+            pltpu.VMEM((SLOTS + 2, 2, CELLS, 384), F32),
+            pltpu.VMEM((SLOTS, 2, CELLS, 128), F32), dma(5), dma(5),
         ],
         compiler_params=PARAMS,
         cost_estimate=cost(10**9, 8 << 20),
-    )(row_counts, displacement, above, below, stiffness, coupling, softening, biased)
+    )(row_counts, displacement, stiffness, coupling, softening, biased)
 
 
 def per_device(
@@ -504,20 +524,18 @@
     devices = lax.axis_size("row")
     up = [(i, i + 1) for i in range(devices - 1)]
     down = [(j, i) for i, j in up]
-    first, last = edge_rows(displacement, row_counts)
+    sent, first, last = forward(displacement, row_counts, table, turns)
     above = lax.ppermute(last, "row", up)
     below = lax.ppermute(first, "row", down)
-    sent = forward(displacement, table, turns)
-    sent, above, below = lax.optimization_barrier((sent, above, below))
     received = lax.all_to_all(sent, "row", split_axis=0, concat_axis=0, tiled=True)
+    couple = jnp.broadcast_to(coupling[None, :], (2, 384))
     structural, part = structure(
-        displacement, above, below, stiffness, coupling[None, :], softening[None, :],
+        displacement, stiffness, coupling[None, :], softening[None, :],
         electrode_mask.astype(F32).T, row_counts,
     )
-    received, structural, part = lax.optimization_barrier((received, structural, part))
     sent = middle(received, row_counts, table, turns, green_spectrum)
     received = lax.all_to_all(sent, "row", split_axis=0, concat_axis=0, tiled=True)
-    return backward(received, structural, part, table, turns)
+    return backward(received, structural, part, above, below, couple, row_counts, table, turns)
 
 
 def solution(mesh):

time: 90.5 us -> 82.5 us (0.912)
  the two profiles are of different devices: /device:TPU:1 before, /device:TPU:24 now
where the time goes in v3:
time: 82.5 us; the launch traced here: 82.1 us
  blocking collectives  28.6 us (35%)
  Pallas kernels  27.3 us (33%)
  starting transfers between devices  15.7 us (19%)
  waiting for transfers between devices  6.88 us (8%)
  local copies, waits for them, and re-layouts  3.48 us (4%)
    all_to_all x1, blocking collectives, per_device(): lax.all_to_all(sent, 'row', split_axis=0, concat_axis=0, tiled=True)  28.6 us
    ppermute x1, starting transfers between devices, per_device(): below = lax.ppermute(first, 'row', down)  7.9 us
    pallas_call x1, Pallas kernels, backward(): pl.pallas_call(backward_kernel, in_specs=[SCALARS] + [HBM] * 9, out_specs...  7.77 us
    pallas_call x1, Pallas kernels, structure(): pl.pallas_call(structural_kernel, in_specs=[SCALARS] + [HBM] * 2 + [VECTO...  7.09 us
    ppermute x1, waiting for transfers between devices, per_device(): above = lax.ppermute(last, 'row', up)  6.87 us
    pallas_call x1, Pallas kernels, middle(): pl.pallas_call(middle_kernel, in_specs=[SCALARS] + [HBM] * 4, out_specs=H...  6.67 us
    all_to_all x1, starting transfers between devices, per_device(): lax.all_to_all(sent, 'row', split_axis=0, concat_axis=0, tiled=True)  5.76 us
    pallas_call x1, Pallas kernels, forward(): pl.pallas_call(forward_kernel, in_specs=[SCALARS] + [HBM] * 4, out_specs=...  5.73 us
  transfers between devices with their start and end apart: 3, of which 1 were waited for; matrix products, arithmetic and copies ran while one was open for 2% of the time, Pallas kernels for 9%

profile of v3, /device:TPU:24, one launch (start us, length us, event | category | flops | bytes accessed | tf_op | source)
XLA Modules:
  0.0 82.1 jit_solution(14531320646327586809)
XLA Ops:
  0.0 5.7 %shard_map.109 = (f32[8,16,16,128]{3,2,1,0:T(8,128)}, f32[1,256,2,384]{3,2,1,0:T(2,128)}, f32[1,256,2,384]{3,2,1,0:T(2,128)}) custom-call(s32[128]{0:T(128)} %counts_ref.7, f32[4,256,2,384]{3,2,1,0:T(2,128)} %x_hbm.3, bf16[256,512]{1,0:T(8,128)(2,1)} %constant.10.clone.order_hbm, bf16[2,512,512]{2,1,0:T(8,128)(2,1)} %constant.8.clone.table_hbm, ...), custom_call_target="tpu_custom_call" | custom-call | flops 1000000000 | bytes 7340032 | tf_op jit(solution)/shard_map/pallas_call | solution.py:441
  5.7 28.6 %all_to_all.10 = f32[128,16,128]{2,1,0:T(8,128)} all-to-all(f32[128,16,128]{2,1,0:T(8,128)} %bitcast.7), channel_id=1, replica_groups=mesh['row'=128] {'row'}, dimensions={0} | all-to-all | bytes 2097152 | tf_op jit(solution)/shard_map/all_to_all | solution.py:530
  34.3 0.0 copy-start.6
  34.3 0.0 copy-start.5
  34.3 0.0 copy-start.3
  34.3 0.0 copy-start.4
  34.3 6.7 %shard_map.110 = f32[128,2,4,2,128]{4,3,2,1,0:T(2,128)} custom-call(s32[128]{0:T(128)} %counts_ref.7, f32[128,2,4,2,128]{4,3,2,1,0:T(2,128)} %bitcast.8, bf16[2,512,512]{2,1,0:T(8,128)(2,1)} %constant.8.clone.table_hbm, f32[16,512]{1,0:T(8,128)} %constant.9.clone.twist_hbm, f32[32,4096]{1,0:T(8,128)} %green_hbm.1), custom_call_target="tpu_custom_call" | custom-call | flops 3000000000 | bytes 5242880 | tf_op jit(solution)/shard_map/pallas_call | solution.py:462
  41.0 5.8 %all-to-all-start.1 = ((f32[128,16,128]{2,1,0:T(8,128)}), f32[128,16,128]{2,1,0:T(8,128)S(1)}, u32[]{:S(2)}, u32[]{:S(2)}) async-start(f32[128,16,128]{2,1,0:T(8,128)} %bitcast.6), calls=%async_computation.1 | async-start | bytes 2097152 | tf_op jit(solution)/shard_map/all_to_all | solution.py:537
  46.7 2.1 %collective-permute-start = (f32[1,256,2,384]{3,2,1,0:T(2,128)}, f32[1,256,2,384]{3,2,1,0:T(2,128)S(1)}, u32[]{:S(2)}, u32[]{:S(2)}) collective-permute-start(f32[1,256,2,384]{3,2,1,0:T(2,128)} %get-tuple-element.13), channel_id=1, source_target_pairs={{0,1},{1,2},{2,3},{3,4},{4,5},{5,6},{6,7},{7,8},{8,9},{9,10},{10,1... | collective-permute-start | bytes 2359304 | tf_op jit(solution)/shard_map/ppermute | solution.py:528
  48.8 0.0 copy-done.6
  48.8 7.9 %collective-permute-start.1 = (f32[1,256,2,384]{3,2,1,0:T(2,128)S(1)}, f32[1,256,2,384]{3,2,1,0:T(2,128)S(1)}, u32[]{:S(2)}, u32[]{:S(2)}) collective-permute-start(f32[1,256,2,384]{3,2,1,0:T(2,128)S(1)} %copy-done.6), channel_id=1, source_target_pairs={{1,0},{2,1},{3,2},{4,3},{5,4},{6,5},{7,6},{8,7},{9,8},{10,9},{11,1... | collective-permute-start | bytes 2359304 | tf_op jit(solution)/shard_map/ppermute | solution.py:529
  56.7 0.0 copy-done.5
  56.7 0.6 broadcast_in_dim.13.soft_ref
  57.3 0.0 copy-done.3
  57.3 0.6 broadcast_in_dim.12.couple_ref
  57.9 0.0 copy-done.4
  57.9 0.8 copy.13
  58.7 7.1 %shard_map.111 = (f32[4,256,2,384]{3,2,1,0:T(2,128)}, f32[4,2,256,128]{3,2,1,0:T(8,128)}) custom-call(s32[128]{0:T(128)} %counts_ref.7, f32[4,256,2,384]{3,2,1,0:T(2,128)} %x_hbm.3, bf16[384,384]{1,0:T(8,128)(2,1)} %stiff_hbm.1, f32[1,384]{1,0:T(1,128)} %broadcast_in_dim.12.couple_ref, f32[1,384]{1,0:T(1,128)} %broadcast_in_dim.13.soft_ref, f32[256,4]{1,0:T(8,128)} %bitcast.9), custom_call_target="tpu_custom_call" | custom-call | flops 1000000000 | bytes 8388608 | tf_op jit(solution)/shard_map/pallas_call | solution.py:501
  65.8 6.9 %collective-permute-done.above_hbm = f32[1,256,2,384]{3,2,1,0:T(2,128)S(1)} collective-permute-done((f32[1,256,2,384]{3,2,1,0:T(2,128)}, f32[1,256,2,384]{3,2,1,0:T(2,128)S(1)}, u32[]{:S(2)}, u32[]{:S(2)}) %collective-permute-start) | collective-permute-done | bytes 786464 | tf_op jit(solution)/shard_map/ppermute | solution.py:528
  72.7 0.0 copy-start.1
  72.7 0.0 collective-permute-done.1.below_hbm
  72.7 0.0 copy-start.2
  72.7 0.0 all-to-all-done.1
  72.7 0.0 copy-start
  72.7 0.6 broadcast_in_dim.14.couple_hbm
  73.4 0.2 copy-done.1
  73.6 0.3 copy-done.2
  73.9 0.3 copy-done
  74.2 7.8 %shard_map.112 = f32[4,256,2,384]{3,2,1,0:T(2,128)} custom-call(s32[128]{0:T(128)} %counts_ref.7, f32[8,16,16,128]{3,2,1,0:T(8,128)} %bitcast.5, f32[4,256,2,384]{3,2,1,0:T(2,128)} %get-tuple-element.11.whole_hbm, f32[4,2,256,128]{3,2,1,0:T(8,128)} %get-tuple-element.12.part_hbm, f32[1,256,2,384]{3,2,1,0:T(2,128)} %copy-done.1, ...), custom_call_target="tpu_custom_call", output_to_operand_aliasing={{}: (2, {})} | custom-call | flops 1000000000 | bytes 8388608 | tf_op jit(solution)/shard_map/pallas_call | solution.py:480
  (1 shorter events, 0.0 us)
Async XLA Ops:
  34.3 14.5 %copy-start.6 = (f32[1,256,2,384]{3,2,1,0:T(2,128)S(1)}, f32[1,256,2,384]{3,2,1,0:T(2,128)}, u32[]{:S(2)}) copy-start(f32[1,256,2,384]{3,2,1,0:T(2,128)} %get-tuple-element.14) | copy-start | bytes 2359300
  34.3 22.4 %copy-start.5 = (f32[384]{0:T(512)S(1)}, f32[384]{0:T(512)}, u32[]{:S(2)}) copy-start(f32[384]{0:T(512)} %param.14) | copy-start | bytes 4612
  34.3 23.0 %copy-start.3 = (f32[384]{0:T(512)S(1)}, f32[384]{0:T(512)}, u32[]{:S(2)}) copy-start(f32[384]{0:T(512)} %param.13) | copy-start | bytes 4612
  34.3 23.6 %copy-start.4 = (s32[4,256]{1,0:T(4,128)S(1)}, s32[4,256]{1,0:T(4,128)}, u32[]{:S(2)}) copy-start(s32[4,256]{1,0:T(4,128)} %param.15) | copy-start | bytes 12292
  41.0 31.7 %all-to-all-start.1 = ((f32[128,16,128]{2,1,0:T(8,128)}), f32[128,16,128]{2,1,0:T(8,128)S(1)}, u32[]{:S(2)}, u32[]{:S(2)}) async-start(f32[128,16,128]{2,1,0:T(8,128)} %bitcast.6), calls=%async_computation.1 | async-start | bytes 2097152 | tf_op jit(solution)/shard_map/all_to_all | solution.py:537
  46.7 26.0 %collective-permute-start = (f32[1,256,2,384]{3,2,1,0:T(2,128)}, f32[1,256,2,384]{3,2,1,0:T(2,128)S(1)}, u32[]{:S(2)}, u32[]{:S(2)}) collective-permute-start(f32[1,256,2,384]{3,2,1,0:T(2,128)} %get-tuple-element.13), channel_id=1, source_target_pairs={{0,1},{1,2},{2,3},{3,4},{4,5},{5,6},{6,7},{7,8},{8,9},{9,10},{10,1... | collective-permute-start | bytes 2359304 | tf_op jit(solution)/shard_map/ppermute | solution.py:528
  48.8 23.9 %collective-permute-start.1 = (f32[1,256,2,384]{3,2,1,0:T(2,128)S(1)}, f32[1,256,2,384]{3,2,1,0:T(2,128)S(1)}, u32[]{:S(2)}, u32[]{:S(2)}) collective-permute-start(f32[1,256,2,384]{3,2,1,0:T(2,128)S(1)} %copy-done.6), channel_id=1, source_target_pairs={{1,0},{2,1},{3,2},{4,3},{5,4},{6,5},{7,6},{8,7},{9,8},{10,9},{11,1... | collective-permute-start | bytes 2359304 | tf_op jit(solution)/shard_map/ppermute | solution.py:529
  72.7 0.9 %copy-start.1 = (f32[1,256,2,384]{3,2,1,0:T(2,128)}, f32[1,256,2,384]{3,2,1,0:T(2,128)S(1)}, u32[]{:S(2)}) copy-start(f32[1,256,2,384]{3,2,1,0:T(2,128)S(1)} %collective-permute-done.above_hbm) | copy-start | bytes 2359300
  72.7 1.2 %copy-start.2 = (f32[1,256,2,384]{3,2,1,0:T(2,128)}, f32[1,256,2,384]{3,2,1,0:T(2,128)S(1)}, u32[]{:S(2)}) copy-start(f32[1,256,2,384]{3,2,1,0:T(2,128)S(1)} %collective-permute-done.1.below_hbm) | copy-start | bytes 2359300
  72.7 1.5 %copy-start = (f32[128,16,128]{2,1,0:T(8,128)}, f32[128,16,128]{2,1,0:T(8,128)S(1)}, u32[]{:S(2)}) copy-start(f32[128,16,128]{2,1,0:T(8,128)S(1)} %all-to-all-done.1) | copy-start | bytes 3145732

commit v4 on v3

--- a/solution.py
+++ b/solution.py
@@ -145,20 +145,23 @@
 
 
 def forward_kernel(
-    counts_ref, x_hbm, order_hbm, table_hbm, twist_hbm, out_hbm, first_hbm, last_hbm,
-    x_ref, order_ref, table_ref, twist_ref, out_ref, first_ref, last_ref, y_ref, sems, out_sems,
+    counts_hbm, x_hbm, order_hbm, table_hbm, twist_hbm, out_hbm, first_hbm, last_hbm,
+    counts_ref, x_ref, order_ref, table_ref, twist_ref, out_ref, first_ref, last_ref, y_ref,
+    sems, out_sems,
 ):
-    count = counts_ref[lax.axis_index("row")]
     copies = fetch(
         (
-            order_hbm, x_hbm.at[:, :, :, 0:128], table_hbm, twist_hbm,
-            x_hbm.at[0:1], x_hbm.at[pl.ds(count - 1, 1)],
+            counts_hbm, x_hbm.at[:, :, :, 0:128], order_hbm, table_hbm, twist_hbm,
+            x_hbm.at[0:1],
         ),
-        (order_ref, x_ref, table_ref, twist_ref, first_ref, last_ref),
+        (counts_ref, x_ref, order_ref, table_ref, twist_ref, first_ref),
         sems,
     )
     copies[0].wait()
+    count = counts_ref[lax.axis_index("row")]
+    copies += fetch((x_hbm.at[pl.ds(count - 1, 1)],), (last_ref,), sems.at[pl.ds(6, 1)])
     copies[1].wait()
+    copies[2].wait()
     planes = []
     for c in range(2):
         plane = jnp.concatenate([x_ref[slot, :, c, :] for slot in range(SLOTS)], axis=1)
@@ -168,13 +171,14 @@
     stacked = jnp.concatenate(
         [jnp.concatenate([w0, w1], axis=1), jnp.concatenate([w1, -w0], axis=1)], axis=0
     )
-    copies[2].wait()
-    y_ref[...] = dot3(stacked, table_ref)
     copies[3].wait()
+    for cut in (slice(0, 256), slice(256, 512)):
+        y_ref[:, cut] = dot3(stacked, table_ref.at[:, :, cut])
+    copies[4].wait()
     lane = lax.broadcasted_iota(jnp.int32, (64, 128), 1)
     outs = []
     for n, (held, target) in enumerate(((first_ref, first_hbm), (last_ref, last_hbm))):
-        copies[4 + n].wait()
+        copies[5 + n].wait()
         copy = pltpu.make_async_copy(held, target, out_sems.at[4 + n])
         copy.start()
         outs.append(copy)
@@ -206,12 +210,15 @@
 
 
 def middle_kernel(
-    counts_ref, x_hbm, table_hbm, twist_hbm, green_hbm, out_hbm,
-    x_ref, table_ref, twist_ref, green_ref, out_ref, cells_ref, y_ref, sems, out_sems,
+    counts_hbm, x_hbm, table_hbm, twist_hbm, green_hbm, out_hbm,
+    counts_ref, x_ref, table_ref, twist_ref, green_ref, out_ref, cells_ref, y_ref, sems, out_sems,
 ):
     copies = fetch(
-        (x_hbm, table_hbm, twist_hbm, green_hbm), (x_ref, table_ref, twist_ref, green_ref), sems
-    )
+        (x_hbm, table_hbm, twist_hbm, green_hbm, counts_hbm),
+        (x_ref, table_ref, twist_ref, green_ref, counts_ref),
+        sems,
+    )
+    copies[4].wait()
     copies[0].wait()
 
     def gather(device, start):
@@ -228,9 +235,11 @@
         [jnp.concatenate([w[0], w[1]], axis=1), jnp.concatenate([w[1], -w[0]], axis=1)], axis=0
     )
     copies[1].wait()
-    y_ref[...] = dot3(stacked, table_ref)
+    for cut in (slice(0, 256), slice(256, 512)):
+        y_ref[:, cut] = dot3(stacked, table_ref.at[:, :, cut])
     copies[2].wait()
     copies[3].wait()
+    back = 0.0
     for lane_tile in range(4):
         cut = slice(lane_tile * 128, lane_tile * 128 + 128)
         for row in range(4):
@@ -252,7 +261,9 @@
                     value = twist(value, twist_ref[a:a + 1, cut], twist_ref[8 + a:9 + a, cut], 1)
                 for o in range(2):
                     tile(y_ref, o, block, row, lane_tile)[...] = value[o]
-    back = inverse_cells(y_ref, table_ref)
+        if lane_tile % 2:
+            half = slice(lane_tile * 128 - 128, lane_tile * 128 + 128)
+            back = back + inverse_cells(y_ref, table_ref, half)
     for c in range(2):
         cells_ref[c, CELLS:] = jnp.zeros((8, 2, 128), F32)
         for h in range(2):
@@ -280,39 +291,44 @@
         copy.wait()
 
 
-def inverse_cells(y_ref, table_ref):
-    re, im = y_ref[0:256, :], y_ref[256:512, :]
+def inverse_cells(y_ref, table_ref, cut):
+    re, im = y_ref[0:256, cut], y_ref[256:512, cut]
     by_cos = jnp.concatenate([re, im], axis=0)
     by_sin = jnp.concatenate([-im, re], axis=0)
-    return dot3_nt(table_ref[0, 0:256, :], table_ref[1, 0:256, :], by_cos) + dot3_nt(
-        table_ref[0, 256:512, :], table_ref[1, 256:512, :], by_sin
+    return dot3_nt(table_ref[0, 0:256, cut], table_ref[1, 0:256, cut], by_cos) + dot3_nt(
+        table_ref[0, 256:512, cut], table_ref[1, 256:512, cut], by_sin
     )
 
 
 def backward_kernel(
-    counts_ref, x_hbm, whole_hbm, part_hbm, above_hbm, below_hbm, couple_hbm, order_hbm,
+    counts_hbm, x_hbm, whole_hbm, part_hbm, above_hbm, below_hbm, couple_hbm, order_hbm,
     table_hbm, twist_hbm, out_hbm,
-    x_ref, part_ref, above_ref, below_ref, couple_ref, first_ref, last_ref, order_ref,
+    counts_ref, x_ref, part_ref, above_ref, below_ref, couple_ref, first_ref, last_ref, order_ref,
     table_ref, twist_ref, out_ref, y_ref, sems, out_sems,
 ):
-    count = counts_ref[lax.axis_index("row")]
     rest = slice(128, 384)
     first_row = whole_hbm.at[0, :, :, rest]
-    last_row = whole_hbm.at[count - 1, :, :, rest]
     copies = fetch(
         (
             x_hbm, twist_hbm, table_hbm, order_hbm, part_hbm,
-            above_hbm, below_hbm, couple_hbm, first_row, last_row,
+            above_hbm, below_hbm, couple_hbm, first_row, counts_hbm,
         ),
         (
             x_ref, twist_ref, table_ref, order_ref, part_ref,
-            above_ref, below_ref, couple_ref, first_ref, last_ref,
+            above_ref, below_ref, couple_ref, first_ref, counts_ref,
         ),
         sems,
+    )
+    copies.pop().wait()
+    count = counts_ref[lax.axis_index("row")]
+    copies += fetch(
+        (whole_hbm.at[count - 1, :, :, rest],), (last_ref,), sems.at[pl.ds(10, 1)]
     )
     lane = lax.broadcasted_iota(jnp.int32, (64, 128), 1)
     copies[0].wait()
     copies[1].wait()
+    copies[2].wait()
+    back = 0.0
     for lane_tile in range(4):
         cut = slice(lane_tile * 128, lane_tile * 128 + 128)
         for o in range(2):
@@ -332,8 +348,9 @@
                     value = twist(value, twist_ref[b:b + 1, cut], twist_ref[8 + b:9 + b, cut], 1)
                 for o in range(2):
                     tile(y_ref, o, b, row, lane_tile)[...] = value[o]
-    copies[2].wait()
-    back = inverse_cells(y_ref, table_ref)
+        if lane_tile % 2:
+            half = slice(lane_tile * 128 - 128, lane_tile * 128 + 128)
+            back = back + inverse_cells(y_ref, table_ref, half)
     copies[3].wait()
     for copy in copies[4:]:
         copy.wait()
@@ -365,10 +382,13 @@
         )
         copy.start()
         outs.append(copy)
-    last_copy.wait()
-    copy = pltpu.make_async_copy(first_ref, out_hbm.at[0, :, :, rest], out_sems.at[SLOTS + 1])
-    copy.start()
-    outs.append(copy)
+        if slot == 1:
+            last_copy.wait()
+            copy = pltpu.make_async_copy(
+                first_ref, out_hbm.at[0, :, :, rest], out_sems.at[SLOTS + 1]
+            )
+            copy.start()
+            outs.append(copy)
     for copy in outs:
         copy.wait()
 
@@ -419,6 +439,7 @@
 SCALARS = pl.BlockSpec(memory_space=pltpu.SMEM)
 VECTORS = pl.BlockSpec(memory_space=pltpu.VMEM)
 CHUNK = (DEVICES, 16, 128)
+COUNTS = pltpu.SMEM((DEVICES,), jnp.int32)
 ORDER = pltpu.VMEM((256, 512), BF16)
 TABLE = pltpu.VMEM((2, 512, 512), BF16)
 TURNS = pltpu.VMEM((16, 512), F32)
@@ -440,7 +461,7 @@
     shape = (8, 16, 16, 128)
     sent, first, last = pl.pallas_call(
         forward_kernel,
-        in_specs=[SCALARS] + [HBM] * 4,
+        in_specs=[HBM] * 5,
         out_specs=[HBM] * 3,
         out_shape=[
             jax.ShapeDtypeStruct(shape, F32),
@@ -448,8 +469,9 @@
             jax.ShapeDtypeStruct(EDGE, F32),
         ],
         scratch_shapes=[
-            pltpu.VMEM((SLOTS, CELLS, 2, 128), F32), ORDER, TABLE, TURNS, pltpu.VMEM(shape, F32),
-            pltpu.VMEM(EDGE, F32), pltpu.VMEM(EDGE, F32), SPECTRAL, dma(6), dma(6),
+            COUNTS, pltpu.VMEM((SLOTS, CELLS, 2, 128), F32), ORDER, TABLE, TURNS,
+            pltpu.VMEM(shape, F32),
+            pltpu.VMEM(EDGE, F32), pltpu.VMEM(EDGE, F32), SPECTRAL, dma(7), dma(6),
         ],
         compiler_params=PARAMS,
         cost_estimate=cost(10**9, 7 << 20),
@@ -461,13 +483,13 @@
     shape = (DEVICES, 2, SLOTS, 2, 128)
     sent = pl.pallas_call(
         middle_kernel,
-        in_specs=[SCALARS] + [HBM] * 4,
+        in_specs=[HBM] * 5,
         out_specs=HBM,
         out_shape=jax.ShapeDtypeStruct(shape, F32),
         scratch_shapes=[
-            pltpu.VMEM(shape, F32), TABLE, TURNS, pltpu.VMEM((32, PAD), F32),
+            COUNTS, pltpu.VMEM(shape, F32), TABLE, TURNS, pltpu.VMEM((32, PAD), F32),
             pltpu.VMEM(shape, F32), pltpu.VMEM((2, CELLS + 8, 2, 128), F32), SPECTRAL,
-            dma(4), dma(4),
+            dma(5), dma(4),
         ],
         compiler_params=PARAMS,
         cost_estimate=cost(3 * 10**9, 5 << 20),
@@ -479,14 +501,14 @@
     edge = pltpu.VMEM((CELLS, 2, 256), F32)
     return pl.pallas_call(
         backward_kernel,
-        in_specs=[SCALARS] + [HBM] * 9,
+        in_specs=[HBM] * 10,
         out_specs=HBM,
         out_shape=jax.ShapeDtypeStruct(BLOCK, F32),
         scratch_shapes=[
-            pltpu.VMEM((8, 16, 16, 128), F32), pltpu.VMEM((SLOTS, 2, CELLS, 128), F32),
+            COUNTS, pltpu.VMEM((8, 16, 16, 128), F32), pltpu.VMEM((SLOTS, 2, CELLS, 128), F32),
             pltpu.VMEM(EDGE, F32), pltpu.VMEM(EDGE, F32), pltpu.VMEM((2, 384), F32), edge, edge,
             ORDER, TABLE, TURNS, pltpu.VMEM((SLOTS, CELLS, 2, 128), F32), SPECTRAL,
-            dma(10), dma(SLOTS + 2),
+            dma(11), dma(SLOTS + 2),
         ],
         input_output_aliases={2: 0},
         compiler_params=PARAMS,

time: 82.5 us -> 80.2 us (0.972)
  Pallas kernels: 27.3 us -> 25 us
    pallas_call x3, Pallas kernels: 20.2 us -> 17.9 us  [the longest x1 6.98 us: backward(): pl.pallas_call(backward_kernel, in_specs=[HBM] * 10, out_specs=HBM, out_s...]
where the time goes in v4:
time: 80.2 us; the launch traced here: 79.9 us
  blocking collectives  28.5 us (36%)
  Pallas kernels  25 us (31%)
  starting transfers between devices  15.7 us (20%)
  waiting for transfers between devices  6.87 us (9%)
  local copies, waits for them, and re-layouts  3.48 us (4%)
    all_to_all x1, blocking collectives, per_device(): lax.all_to_all(sent, 'row', split_axis=0, concat_axis=0, tiled=True)  28.5 us
    ppermute x1, starting transfers between devices, per_device(): below = lax.ppermute(first, 'row', down)  7.9 us
    pallas_call x1, Pallas kernels, structure(): pl.pallas_call(structural_kernel, in_specs=[SCALARS] + [HBM] * 2 + [VECTO...  7.09 us
    pallas_call x1, Pallas kernels, backward(): pl.pallas_call(backward_kernel, in_specs=[HBM] * 10, out_specs=HBM, out_s...  6.98 us
    ppermute x1, waiting for transfers between devices, per_device(): above = lax.ppermute(last, 'row', up)  6.87 us
    pallas_call x1, Pallas kernels, middle(): pl.pallas_call(middle_kernel, in_specs=[HBM] * 5, out_specs=HBM, out_shap...  5.89 us
    all_to_all x1, starting transfers between devices, per_device(): lax.all_to_all(sent, 'row', split_axis=0, concat_axis=0, tiled=True)  5.76 us
    pallas_call x1, Pallas kernels, forward(): pl.pallas_call(forward_kernel, in_specs=[HBM] * 5, out_specs=[HBM] * 3, o...  5.03 us
  transfers between devices with their start and end apart: 3, of which 1 were waited for; matrix products, arithmetic and copies ran while one was open for 2% of the time, Pallas kernels for 9%

profile of v4, /device:TPU:24, one launch (start us, length us, event | category | flops | bytes accessed | tf_op | source)
XLA Modules:
  0.0 79.9 jit_solution(16041960170187770095)
XLA Ops:
  0.0 5.0 %shard_map.109 = (f32[8,16,16,128]{3,2,1,0:T(8,128)}, f32[1,256,2,384]{3,2,1,0:T(2,128)}, f32[1,256,2,384]{3,2,1,0:T(2,128)}) custom-call(s32[128]{0:T(128)} %counts_hbm.5, f32[4,256,2,384]{3,2,1,0:T(2,128)} %x_hbm.3, bf16[256,512]{1,0:T(8,128)(2,1)} %constant.10.clone.order_hbm, bf16[2,512,512]{2,1,0:T(8,128)(2,1)} %constant.8.clone.table_hbm, ...), custom_call_target="tpu_custom_call" | custom-call | flops 1000000000 | bytes 7340032 | tf_op jit(solution)/shard_map/pallas_call | solution.py:462
  5.0 28.5 %all_to_all.10 = f32[128,16,128]{2,1,0:T(8,128)} all-to-all(f32[128,16,128]{2,1,0:T(8,128)} %bitcast.7), channel_id=1, replica_groups=mesh['row'=128] {'row'}, dimensions={0} | all-to-all | bytes 2097152 | tf_op jit(solution)/shard_map/all_to_all | solution.py:552
  33.6 0.0 copy-start.6
  33.6 0.0 copy-start.5
  33.6 0.0 copy-start.3
  33.6 0.0 copy-start.4
  33.6 5.9 %shard_map.110 = f32[128,2,4,2,128]{4,3,2,1,0:T(2,128)} custom-call(s32[128]{0:T(128)} %counts_hbm.5, f32[128,2,4,2,128]{4,3,2,1,0:T(2,128)} %bitcast.8, bf16[2,512,512]{2,1,0:T(8,128)(2,1)} %constant.8.clone.table_hbm, f32[16,512]{1,0:T(8,128)} %constant.9.clone.twist_hbm, f32[32,4096]{1,0:T(8,128)} %green_hbm.1), custom_call_target="tpu_custom_call" | custom-call | flops 3000000000 | bytes 5242880 | tf_op jit(solution)/shard_map/pallas_call | solution.py:484
  39.5 5.8 %all-to-all-start.1 = ((f32[128,16,128]{2,1,0:T(8,128)}), f32[128,16,128]{2,1,0:T(8,128)S(1)}, u32[]{:S(2)}, u32[]{:S(2)}) async-start(f32[128,16,128]{2,1,0:T(8,128)} %bitcast.6), calls=%async_computation.1 | async-start | bytes 2097152 | tf_op jit(solution)/shard_map/all_to_all | solution.py:559
  45.3 2.1 %collective-permute-start = (f32[1,256,2,384]{3,2,1,0:T(2,128)}, f32[1,256,2,384]{3,2,1,0:T(2,128)S(1)}, u32[]{:S(2)}, u32[]{:S(2)}) collective-permute-start(f32[1,256,2,384]{3,2,1,0:T(2,128)} %get-tuple-element.13), channel_id=1, source_target_pairs={{0,1},{1,2},{2,3},{3,4},{4,5},{5,6},{6,7},{7,8},{8,9},{9,10},{10,1... | collective-permute-start | bytes 2359304 | tf_op jit(solution)/shard_map/ppermute | solution.py:550
  47.3 0.0 copy-done.6
  47.4 7.9 %collective-permute-start.1 = (f32[1,256,2,384]{3,2,1,0:T(2,128)S(1)}, f32[1,256,2,384]{3,2,1,0:T(2,128)S(1)}, u32[]{:S(2)}, u32[]{:S(2)}) collective-permute-start(f32[1,256,2,384]{3,2,1,0:T(2,128)S(1)} %copy-done.6), channel_id=1, source_target_pairs={{1,0},{2,1},{3,2},{4,3},{5,4},{6,5},{7,6},{8,7},{9,8},{10,9},{11,1... | collective-permute-start | bytes 2359304 | tf_op jit(solution)/shard_map/ppermute | solution.py:551
  55.3 0.0 copy-done.5
  55.3 0.6 broadcast_in_dim.13.soft_ref
  55.9 0.0 copy-done.3
  55.9 0.6 broadcast_in_dim.12.couple_ref
  56.4 0.0 copy-done.4
  56.5 0.8 %copy.13 = f32[4,256]{0,1:T(8,128)} copy(f32[4,256]{1,0:T(4,128)S(1)} %convert_element_type.3) | data formatting | bytes 8192 | tf_op jit(solution)/shard_map/convert_element_type | solution.py:556
  57.3 7.1 %shard_map.111 = (f32[4,256,2,384]{3,2,1,0:T(2,128)}, f32[4,2,256,128]{3,2,1,0:T(8,128)}) custom-call(s32[128]{0:T(128)} %counts_hbm.5, f32[4,256,2,384]{3,2,1,0:T(2,128)} %x_hbm.3, bf16[384,384]{1,0:T(8,128)(2,1)} %stiff_hbm.1, f32[1,384]{1,0:T(1,128)} %broadcast_in_dim.12.couple_ref, f32[1,384]{1,0:T(1,128)} %broadcast_in_dim.13.soft_ref, f32[256,4]{1,0:T(8,128)} %bitcast.9), custom_call_target="tpu_custom_call" | custom-call | flops 1000000000 | bytes 8388608 | tf_op jit(solution)/shard_map/pallas_call | solution.py:523
  64.4 6.9 %collective-permute-done.above_hbm = f32[1,256,2,384]{3,2,1,0:T(2,128)S(1)} collective-permute-done((f32[1,256,2,384]{3,2,1,0:T(2,128)}, f32[1,256,2,384]{3,2,1,0:T(2,128)S(1)}, u32[]{:S(2)}, u32[]{:S(2)}) %collective-permute-start) | collective-permute-done | bytes 786464 | tf_op jit(solution)/shard_map/ppermute | solution.py:550
  71.2 0.0 copy-start.1
  71.2 0.0 collective-permute-done.1.below_hbm
  71.2 0.0 copy-start.2
  71.2 0.0 all-to-all-done.1
  71.2 0.0 copy-start
  71.3 0.6 broadcast_in_dim.14.couple_hbm
  71.9 0.2 copy-done.1
  72.1 0.3 copy-done.2
  72.4 0.3 copy-done
  72.7 7.0 %shard_map.112 = f32[4,256,2,384]{3,2,1,0:T(2,128)} custom-call(s32[128]{0:T(128)} %counts_hbm.5, f32[8,16,16,128]{3,2,1,0:T(8,128)} %bitcast.5, f32[4,256,2,384]{3,2,1,0:T(2,128)} %get-tuple-element.11.whole_hbm, f32[4,2,256,128]{3,2,1,0:T(8,128)} %get-tuple-element.12.part_hbm, f32[1,256,2,384]{3,2,1,0:T(2,128)} %copy-done.1, ...), custom_call_target="tpu_custom_call", output_to_operand_aliasing={{}: (2, {})} | custom-call | flops 1000000000 | bytes 8388608 | tf_op jit(solution)/shard_map/pallas_call | solution.py:502
  (1 shorter events, 0.0 us)
Async XLA Ops:
  33.6 13.8 %copy-start.6 = (f32[1,256,2,384]{3,2,1,0:T(2,128)S(1)}, f32[1,256,2,384]{3,2,1,0:T(2,128)}, u32[]{:S(2)}) copy-start(f32[1,256,2,384]{3,2,1,0:T(2,128)} %get-tuple-element.14) | copy-start | bytes 2359300
  33.6 21.7 %copy-start.5 = (f32[384]{0:T(512)S(1)}, f32[384]{0:T(512)}, u32[]{:S(2)}) copy-start(f32[384]{0:T(512)} %param.14) | copy-start | bytes 4612
  33.6 22.3 %copy-start.3 = (f32[384]{0:T(512)S(1)}, f32[384]{0:T(512)}, u32[]{:S(2)}) copy-start(f32[384]{0:T(512)} %param.13) | copy-start | bytes 4612
  33.6 22.8 %copy-start.4 = (s32[4,256]{1,0:T(4,128)S(1)}, s32[4,256]{1,0:T(4,128)}, u32[]{:S(2)}) copy-start(s32[4,256]{1,0:T(4,128)} %param.15) | copy-start | bytes 12292
  39.5 31.7 %all-to-all-start.1 = ((f32[128,16,128]{2,1,0:T(8,128)}), f32[128,16,128]{2,1,0:T(8,128)S(1)}, u32[]{:S(2)}, u32[]{:S(2)}) async-start(f32[128,16,128]{2,1,0:T(8,128)} %bitcast.6), calls=%async_computation.1 | async-start | bytes 2097152 | tf_op jit(solution)/shard_map/all_to_all | solution.py:559
  45.3 26.0 %collective-permute-start = (f32[1,256,2,384]{3,2,1,0:T(2,128)}, f32[1,256,2,384]{3,2,1,0:T(2,128)S(1)}, u32[]{:S(2)}, u32[]{:S(2)}) collective-permute-start(f32[1,256,2,384]{3,2,1,0:T(2,128)} %get-tuple-element.13), channel_id=1, source_target_pairs={{0,1},{1,2},{2,3},{3,4},{4,5},{5,6},{6,7},{7,8},{8,9},{9,10},{10,1... | collective-permute-start | bytes 2359304 | tf_op jit(solution)/shard_map/ppermute | solution.py:550
  47.4 23.9 %collective-permute-start.1 = (f32[1,256,2,384]{3,2,1,0:T(2,128)S(1)}, f32[1,256,2,384]{3,2,1,0:T(2,128)S(1)}, u32[]{:S(2)}, u32[]{:S(2)}) collective-permute-start(f32[1,256,2,384]{3,2,1,0:T(2,128)S(1)} %copy-done.6), channel_id=1, source_target_pairs={{1,0},{2,1},{3,2},{4,3},{5,4},{6,5},{7,6},{8,7},{9,8},{10,9},{11,1... | collective-permute-start | bytes 2359304 | tf_op jit(solution)/shard_map/ppermute | solution.py:551
  71.2 0.9 %copy-start.1 = (f32[1,256,2,384]{3,2,1,0:T(2,128)}, f32[1,256,2,384]{3,2,1,0:T(2,128)S(1)}, u32[]{:S(2)}) copy-start(f32[1,256,2,384]{3,2,1,0:T(2,128)S(1)} %collective-permute-done.above_hbm) | copy-start | bytes 2359300
  71.2 1.2 %copy-start.2 = (f32[1,256,2,384]{3,2,1,0:T(2,128)}, f32[1,256,2,384]{3,2,1,0:T(2,128)S(1)}, u32[]{:S(2)}) copy-start(f32[1,256,2,384]{3,2,1,0:T(2,128)S(1)} %collective-permute-done.1.below_hbm) | copy-start | bytes 2359300
  71.2 1.5 %copy-start = (f32[128,16,128]{2,1,0:T(8,128)}, f32[128,16,128]{2,1,0:T(8,128)S(1)}, u32[]{:S(2)}) copy-start(f32[128,16,128]{2,1,0:T(8,128)S(1)} %all-to-all-done.1) | copy-start | bytes 3145732

commit v5 on v4

--- a/solution.py
+++ b/solution.py
@@ -210,16 +210,15 @@
 
 
 def middle_kernel(
-    counts_hbm, x_hbm, table_hbm, twist_hbm, green_hbm, out_hbm,
-    counts_ref, x_ref, table_ref, twist_ref, green_ref, out_ref, cells_ref, y_ref, sems, out_sems,
+    counts_hbm, x_ref, table_hbm, twist_hbm, green_hbm, out_hbm,
+    counts_ref, table_ref, twist_ref, green_ref, out_ref, cells_ref, y_ref, sems, out_sems,
 ):
     copies = fetch(
-        (x_hbm, table_hbm, twist_hbm, green_hbm, counts_hbm),
-        (x_ref, table_ref, twist_ref, green_ref, counts_ref),
+        (table_hbm, twist_hbm, green_hbm, counts_hbm),
+        (table_ref, twist_ref, green_ref, counts_ref),
         sems,
     )
-    copies[4].wait()
-    copies[0].wait()
+    copies[3].wait()
 
     def gather(device, start):
         for c in range(2):
@@ -234,11 +233,11 @@
     stacked = jnp.concatenate(
         [jnp.concatenate([w[0], w[1]], axis=1), jnp.concatenate([w[1], -w[0]], axis=1)], axis=0
     )
-    copies[1].wait()
+    copies[0].wait()
     for cut in (slice(0, 256), slice(256, 512)):
         y_ref[:, cut] = dot3(stacked, table_ref.at[:, :, cut])
+    copies[1].wait()
     copies[2].wait()
-    copies[3].wait()
     back = 0.0
     for lane_tile in range(4):
         cut = slice(lane_tile * 128, lane_tile * 128 + 128)
@@ -301,20 +300,20 @@
 
 
 def backward_kernel(
-    counts_hbm, x_hbm, whole_hbm, part_hbm, above_hbm, below_hbm, couple_hbm, order_hbm,
+    counts_hbm, x_ref, whole_hbm, part_hbm, above_hbm, below_hbm, couple_hbm, order_hbm,
     table_hbm, twist_hbm, out_hbm,
-    counts_ref, x_ref, part_ref, above_ref, below_ref, couple_ref, first_ref, last_ref, order_ref,
+    counts_ref, part_ref, above_ref, below_ref, couple_ref, first_ref, last_ref, order_ref,
     table_ref, twist_ref, out_ref, y_ref, sems, out_sems,
 ):
     rest = slice(128, 384)
     first_row = whole_hbm.at[0, :, :, rest]
     copies = fetch(
         (
-            x_hbm, twist_hbm, table_hbm, order_hbm, part_hbm,
+            twist_hbm, table_hbm, order_hbm, part_hbm,
             above_hbm, below_hbm, couple_hbm, first_row, counts_hbm,
         ),
         (
-            x_ref, twist_ref, table_ref, order_ref, part_ref,
+            twist_ref, table_ref, order_ref, part_ref,
             above_ref, below_ref, couple_ref, first_ref, counts_ref,
         ),
         sems,
@@ -322,12 +321,11 @@
     copies.pop().wait()
     count = counts_ref[lax.axis_index("row")]
     copies += fetch(
-        (whole_hbm.at[count - 1, :, :, rest],), (last_ref,), sems.at[pl.ds(10, 1)]
+        (whole_hbm.at[count - 1, :, :, rest],), (last_ref,), sems.at[pl.ds(9, 1)]
     )
     lane = lax.broadcasted_iota(jnp.int32, (64, 128), 1)
     copies[0].wait()
     copies[1].wait()
-    copies[2].wait()
     back = 0.0
     for lane_tile in range(4):
         cut = slice(lane_tile * 128, lane_tile * 128 + 128)
@@ -351,8 +349,8 @@
         if lane_tile % 2:
             half = slice(lane_tile * 128 - 128, lane_tile * 128 + 128)
             back = back + inverse_cells(y_ref, table_ref, half)
-    copies[3].wait()
-    for copy in copies[4:]:
+    copies[2].wait()
+    for copy in copies[3:]:
         copy.wait()
     alone = count == 1
     couple = couple_ref[:, rest]
@@ -483,15 +481,15 @@
     shape = (DEVICES, 2, SLOTS, 2, 128)
     sent = pl.pallas_call(
         middle_kernel,
-        in_specs=[HBM] * 5,
+        in_specs=[HBM, VECTORS] + [HBM] * 3,
         out_specs=HBM,
         out_shape=jax.ShapeDtypeStruct(shape, F32),
         scratch_shapes=[
-            COUNTS, pltpu.VMEM(shape, F32), TABLE, TURNS, pltpu.VMEM((32, PAD), F32),
+            COUNTS, TABLE, TURNS, pltpu.VMEM((32, PAD), F32),
             pltpu.VMEM(shape, F32), pltpu.VMEM((2, CELLS + 8, 2, 128), F32), SPECTRAL,
-            dma(5), dma(4),
+            dma(4), dma(4),
         ],
-        compiler_params=PARAMS,
+        compiler_params=pltpu.CompilerParams(vmem_limit_bytes=40 * 1024 * 1024),
         cost_estimate=cost(3 * 10**9, 5 << 20),
     )(row_counts, received.reshape(shape), table, turns, green_spectrum)
     return sent.reshape(CHUNK)
@@ -501,17 +499,17 @@
     edge = pltpu.VMEM((CELLS, 2, 256), F32)
     return pl.pallas_call(
         backward_kernel,
-        in_specs=[HBM] * 10,
+        in_specs=[HBM, VECTORS] + [HBM] * 8,
         out_specs=HBM,
         out_shape=jax.ShapeDtypeStruct(BLOCK, F32),
         scratch_shapes=[
-            COUNTS, pltpu.VMEM((8, 16, 16, 128), F32), pltpu.VMEM((SLOTS, 2, CELLS, 128), F32),
+            COUNTS, pltpu.VMEM((SLOTS, 2, CELLS, 128), F32),
             pltpu.VMEM(EDGE, F32), pltpu.VMEM(EDGE, F32), pltpu.VMEM((2, 384), F32), edge, edge,
             ORDER, TABLE, TURNS, pltpu.VMEM((SLOTS, CELLS, 2, 128), F32), SPECTRAL,
-            dma(11), dma(SLOTS + 2),
+            dma(10), dma(SLOTS + 2),
         ],
         input_output_aliases={2: 0},
-        compiler_params=PARAMS,
+        compiler_params=pltpu.CompilerParams(vmem_limit_bytes=40 * 1024 * 1024),
         cost_estimate=cost(10**9, 8 << 20),
     )(
         row_counts, received.reshape(8, 16, 16, 128), structural, part, above, below, coupling,

time: 80.2 us -> 78.9 us (0.984)
  Pallas kernels: 25 us -> 23.8 us
    pallas_call x2, Pallas kernels: 12.9 us -> 11.5 us  [the longest x1 6.25 us: backward(): pl.pallas_call(backward_kernel, in_specs=[HBM, VECTORS] + [HBM] * 8, out_...]
  transfers between devices with their start and end apart: 3 -> 3, of which waited for: 1 -> 1; matrix products, arithmetic and copies ran while one was open for 2% -> 3% of each run, Pallas kernels for 9% -> 9%
where the time goes in v5:
time: 78.9 us; the launch traced here: 78.5 us
  blocking collectives  28.4 us (36%)
  Pallas kernels  23.8 us (30%)
  starting transfers between devices  15.9 us (20%)
  waiting for transfers between devices  6.89 us (9%)
  local copies, waits for them, and re-layouts  3.24 us (4%)
    all_to_all x1, blocking collectives, per_device(): lax.all_to_all(sent, 'row', split_axis=0, concat_axis=0, tiled=True)  28.4 us
    ppermute x1, starting transfers between devices, per_device(): below = lax.ppermute(first, 'row', down)  7.91 us
    pallas_call x1, Pallas kernels, structure(): pl.pallas_call(structural_kernel, in_specs=[SCALARS] + [HBM] * 2 + [VECTO...  7.08 us
    ppermute x1, waiting for transfers between devices, per_device(): above = lax.ppermute(last, 'row', up)  6.89 us
    pallas_call x1, Pallas kernels, backward(): pl.pallas_call(backward_kernel, in_specs=[HBM, VECTORS] + [HBM] * 8, out_...  6.25 us
    all_to_all x1, starting transfers between devices, per_device(): lax.all_to_all(sent, 'row', split_axis=0, concat_axis=0, tiled=True)  5.9 us
    pallas_call x1, Pallas kernels, middle(): pl.pallas_call(middle_kernel, in_specs=[HBM, VECTORS] + [HBM] * 3, out_sp...  5.3 us
    pallas_call x1, Pallas kernels, forward(): pl.pallas_call(forward_kernel, in_specs=[HBM] * 5, out_specs=[HBM] * 3, o...  5.15 us
  transfers between devices with their start and end apart: 3, of which 1 were waited for; matrix products, arithmetic and copies ran while one was open for 3% of the time, Pallas kernels for 9%

profile of v5, /device:TPU:24, one launch (start us, length us, event | category | flops | bytes accessed | tf_op | source)
XLA Modules:
  0.0 78.5 jit_solution(114829954887367091)
XLA Ops:
  0.0 0.0 copy-start
  0.0 0.0 copy-start.6
  0.0 5.1 %shard_map.109 = (f32[8,16,16,128]{3,2,1,0:T(8,128)}, f32[1,256,2,384]{3,2,1,0:T(2,128)}, f32[1,256,2,384]{3,2,1,0:T(2,128)}) custom-call(s32[128]{0:T(128)} %counts_hbm.5, f32[4,256,2,384]{3,2,1,0:T(2,128)} %x_hbm.3, bf16[256,512]{1,0:T(8,128)(2,1)} %constant.10.clone.order_hbm, bf16[2,512,512]{2,1,0:T(8,128)(2,1)} %constant.8.clone.table_hbm, ...), custom_call_target="tpu_custom_call" | custom-call | flops 1000000000 | bytes 7340032 | tf_op jit(solution)/shard_map/pallas_call | solution.py:460
  5.2 28.4 %all_to_all.10 = f32[128,16,128]{2,1,0:T(8,128)S(1)} all-to-all(f32[128,16,128]{2,1,0:T(8,128)} %bitcast.7), channel_id=1, replica_groups=mesh['row'=128] {'row'}, dimensions={0} | all-to-all | bytes 2097152 | tf_op jit(solution)/shard_map/all_to_all | solution.py:550
  33.6 0.0 copy-done
  33.6 0.0 copy-done.3
  33.6 0.0 copy-done.4
  33.6 0.0 copy-done.6
  33.6 0.0 copy-start.9
  33.7 0.0 copy-start.7
  33.7 0.0 copy-start.8
  33.7 5.3 %shard_map.110 = f32[128,2,4,2,128]{4,3,2,1,0:T(2,128)} custom-call(s32[128]{0:T(128)S(1)} %copy-done.4, f32[128,2,4,2,128]{4,3,2,1,0:T(2,128)S(1)} %bitcast.6, bf16[2,512,512]{2,1,0:T(8,128)(2,1)S(1)} %copy-done, f32[16,512]{1,0:T(8,128)S(1)} %copy-done.3, f32[32,4096]{1,0:T(8,128)S(1)} %copy-done.6), custom_call_target="tpu_custom_call" | custom-call | flops 3000000000 | bytes 5242880 | tf_op jit(solution)/shard_map/pallas_call | solution.py:482
  39.0 0.0 copy-start.2
  39.0 0.0 copy-start.5
  39.0 5.9 %all-to-all-start.1 = ((f32[128,16,128]{2,1,0:T(8,128)}), f32[128,16,128]{2,1,0:T(8,128)S(1)}, u32[]{:S(2)}, u32[]{:S(2)}) async-start(f32[128,16,128]{2,1,0:T(8,128)} %bitcast.2), calls=%async_computation.1 | async-start | bytes 2097152 | tf_op jit(solution)/shard_map/all_to_all | solution.py:557
  44.9 2.1 %collective-permute-start = (f32[1,256,2,384]{3,2,1,0:T(2,128)}, f32[1,256,2,384]{3,2,1,0:T(2,128)S(1)}, u32[]{:S(2)}, u32[]{:S(2)}) collective-permute-start(f32[1,256,2,384]{3,2,1,0:T(2,128)} %get-tuple-element.13), channel_id=1, source_target_pairs={{0,1},{1,2},{2,3},{3,4},{4,5},{5,6},{6,7},{7,8},{8,9},{9,10},{10,1... | collective-permute-start | bytes 2359304 | tf_op jit(solution)/shard_map/ppermute | solution.py:548
  47.0 7.9 %collective-permute-start.1 = (f32[1,256,2,384]{3,2,1,0:T(2,128)}, f32[1,256,2,384]{3,2,1,0:T(2,128)}, u32[]{:S(2)}, u32[]{:S(2)}) collective-permute-start(f32[1,256,2,384]{3,2,1,0:T(2,128)} %get-tuple-element.14), channel_id=1, source_target_pairs={{1,0},{2,1},{3,2},{4,3},{5,4},{6,5},{7,6},{8,7},{9,8},{10,9},{11,1... | collective-permute-start | bytes 2359304 | tf_op jit(solution)/shard_map/ppermute | solution.py:549
  54.9 0.0 copy-done.9
  54.9 0.6 broadcast_in_dim.13.soft_ref
  55.5 0.0 copy-done.7
  55.5 0.6 broadcast_in_dim.12.couple_ref
  56.1 0.0 copy-done.8
  56.1 0.8 %copy.13 = f32[4,256]{0,1:T(8,128)} copy(f32[4,256]{1,0:T(4,128)S(1)} %convert_element_type.3) | data formatting | bytes 8192 | tf_op jit(solution)/shard_map/convert_element_type | solution.py:554
  56.9 7.1 %shard_map.111 = (f32[4,256,2,384]{3,2,1,0:T(2,128)}, f32[4,2,256,128]{3,2,1,0:T(8,128)}) custom-call(s32[128]{0:T(128)} %counts_hbm.5, f32[4,256,2,384]{3,2,1,0:T(2,128)} %x_hbm.3, bf16[384,384]{1,0:T(8,128)(2,1)} %stiff_hbm.1, f32[1,384]{1,0:T(1,128)} %broadcast_in_dim.12.couple_ref, f32[1,384]{1,0:T(1,128)} %broadcast_in_dim.13.soft_ref, f32[256,4]{1,0:T(8,128)} %bitcast.8), custom_call_target="tpu_custom_call" | custom-call | flops 1000000000 | bytes 8388608 | tf_op jit(solution)/shard_map/pallas_call | solution.py:521
  64.0 6.9 %collective-permute-done.above_hbm = f32[1,256,2,384]{3,2,1,0:T(2,128)S(1)} collective-permute-done((f32[1,256,2,384]{3,2,1,0:T(2,128)}, f32[1,256,2,384]{3,2,1,0:T(2,128)S(1)}, u32[]{:S(2)}, u32[]{:S(2)}) %collective-permute-start) | collective-permute-done | bytes 786464 | tf_op jit(solution)/shard_map/ppermute | solution.py:548
  70.9 0.0 collective-permute-done.1.below_hbm
  70.9 0.0 all-to-all-done.1
  70.9 0.0 copy-done.2
  70.9 0.0 copy-done.5
  70.9 0.0 copy-start.1
  70.9 1.2 %copy-done.1 = f32[4,2,256,128]{3,2,1,0:T(8,128)S(1)} copy-done((f32[4,2,256,128]{3,2,1,0:T(8,128)S(1)}, f32[4,2,256,128]{3,2,1,0:T(8,128)}, u32[]{:S(2)}) %copy-start.1) | copy-done | bytes 1048600
  72.1 6.2 %shard_map.112 = f32[4,256,2,384]{3,2,1,0:T(2,128)} custom-call(s32[128]{0:T(128)S(1)} %copy-done.5, f32[8,16,16,128]{3,2,1,0:T(8,128)S(1)} %bitcast.5, f32[4,256,2,384]{3,2,1,0:T(2,128)} %get-tuple-element.11.whole_hbm, f32[4,2,256,128]{3,2,1,0:T(8,128)S(1)} %copy-done.1, ...), custom_call_target="tpu_custom_call", output_to_operand_aliasing={{}: (2, {})} | custom-call | flops 1000000000 | bytes 8388608 | tf_op jit(solution)/shard_map/pallas_call | solution.py:500
  (4 shorter events, 0.0 us)
Async XLA Ops:
  0.0 33.6 %copy-start = (bf16[2,512,512]{2,1,0:T(8,128)(2,1)S(1)}, bf16[2,512,512]{2,1,0:T(8,128)(2,1)}, u32[]{:S(2)}) copy-start(bf16[2,512,512]{2,1,0:T(8,128)(2,1)} %constant.8.clone.table_hbm) | copy-start | bytes 3145732
  0.0 33.6 %copy-start.3 = (f32[16,512]{1,0:T(8,128)S(1)}, f32[16,512]{1,0:T(8,128)}, u32[]{:S(2)}) copy-start(f32[16,512]{1,0:T(8,128)} %constant.9.clone.twist_hbm) | copy-start | bytes 98308
  0.0 33.6 %copy-start.4 = (s32[128]{0:T(128)S(1)}, s32[128]{0:T(128)}, u32[]{:S(2)}) copy-start(s32[128]{0:T(128)} %counts_hbm.5) | copy-start | bytes 1540
  0.0 33.6 %copy-start.6 = (f32[32,4096]{1,0:T(8,128)S(1)}, f32[32,4096]{1,0:T(8,128)}, u32[]{:S(2)}) copy-start(f32[32,4096]{1,0:T(8,128)} %green_hbm.1) | copy-start | bytes 1572868
  33.6 21.3 %copy-start.9 = (f32[384]{0:T(512)S(1)}, f32[384]{0:T(512)}, u32[]{:S(2)}) copy-start(f32[384]{0:T(512)} %param.14) | copy-start | bytes 4612
  33.7 21.8 %copy-start.7 = (f32[384]{0:T(512)S(1)}, f32[384]{0:T(512)}, u32[]{:S(2)}) copy-start(f32[384]{0:T(512)} %param.13) | copy-start | bytes 4612
  33.7 22.4 %copy-start.8 = (s32[4,256]{1,0:T(4,128)S(1)}, s32[4,256]{1,0:T(4,128)}, u32[]{:S(2)}) copy-start(s32[4,256]{1,0:T(4,128)} %param.15) | copy-start | bytes 12292
  39.0 31.9 %copy-start.2 = (bf16[256,512]{1,0:T(8,128)(2,1)S(1)}, bf16[256,512]{1,0:T(8,128)(2,1)}, u32[]{:S(2)}) copy-start(bf16[256,512]{1,0:T(8,128)(2,1)} %constant.11.clone.order_hbm) | copy-start | bytes 786436
  39.0 31.9 %copy-start.5 = (s32[128]{0:T(128)S(1)}, s32[128]{0:T(128)}, u32[]{:S(2)}) copy-start(s32[128]{0:T(128)} %counts_hbm.5) | copy-start | bytes 1540
  39.0 31.9 %all-to-all-start.1 = ((f32[128,16,128]{2,1,0:T(8,128)}), f32[128,16,128]{2,1,0:T(8,128)S(1)}, u32[]{:S(2)}, u32[]{:S(2)}) async-start(f32[128,16,128]{2,1,0:T(8,128)} %bitcast.2), calls=%async_computation.1 | async-start | bytes 2097152 | tf_op jit(solution)/shard_map/all_to_all | solution.py:557
  44.9 26.0 %collective-permute-start = (f32[1,256,2,384]{3,2,1,0:T(2,128)}, f32[1,256,2,384]{3,2,1,0:T(2,128)S(1)}, u32[]{:S(2)}, u32[]{:S(2)}) collective-permute-start(f32[1,256,2,384]{3,2,1,0:T(2,128)} %get-tuple-element.13), channel_id=1, source_target_pairs={{0,1},{1,2},{2,3},{3,4},{4,5},{5,6},{6,7},{7,8},{8,9},{9,10},{10,1... | collective-permute-start | bytes 2359304 | tf_op jit(solution)/shard_map/ppermute | solution.py:548
  47.0 23.9 %collective-permute-start.1 = (f32[1,256,2,384]{3,2,1,0:T(2,128)}, f32[1,256,2,384]{3,2,1,0:T(2,128)}, u32[]{:S(2)}, u32[]{:S(2)}) collective-permute-start(f32[1,256,2,384]{3,2,1,0:T(2,128)} %get-tuple-element.14), channel_id=1, source_target_pairs={{1,0},{2,1},{3,2},{4,3},{5,4},{6,5},{7,6},{8,7},{9,8},{10,9},{11,1... | collective-permute-start | bytes 2359304 | tf_op jit(solution)/shard_map/ppermute | solution.py:549
  70.9 1.2 %copy-start.1 = (f32[4,2,256,128]{3,2,1,0:T(8,128)S(1)}, f32[4,2,256,128]{3,2,1,0:T(8,128)}, u32[]{:S(2)}) copy-start(f32[4,2,256,128]{3,2,1,0:T(8,128)} %get-tuple-element.12.part_hbm) | copy-start | bytes 3145732
